TPU v7x, 256 devices: a whole 4x4x8 slice. The times are simulated.
256 devices in a mesh: tile: 16 (over x, y), depth: 16 (over z, core).
Axes of the slice: x: 4, y: 4, z: 8, core: 2. Of those that a mesh axis runs over, the one named last changes fastest.
Arguments:
- volume: bfloat16 [16, 16, 128, 128, 128], P('tile', 'depth'), may hold values from -8 to 8
- shear: float32 [16, 16, 2], P('tile', 'depth'), may hold values from -0.5 to 0.5
- absorb: float32 [16, 16], P('tile', 'depth'), may hold values from 0.000390625 to 0.0078125
- color_slope: float32 [3], replicated, may hold values from -3 to 3
- color_bias: float32 [3], replicated, may hold values from -1.5 to 1.5
- frag_tile: int32 [16, 16, 16, 1], P('tile', 'depth'), may hold values from 0 to 15; in each aligned block of 16 rows (0 to 15, 16 to 31, ..., all dimensions but the last counted through in order) at most 4 rows name the same one
- slot_perm: int32 [16, 16, 16, 16], P('tile', 'depth'), may hold values from 0 to 15, each once within a row
- frag_rows: int32 [16, 16, 16], P('tile', 'depth'), may hold values from 1 to 64
- tile_view: int32 [16], replicated, may hold values from 0 to 1
- tile_owner: int32 [16], replicated, may hold values from 0 to 15, each once
Outputs:
- frame: bfloat16 [16, 4, 256, 256], P('tile')
Inputs may be any that keep to these rules, and one draw needn't show every extreme that they name: `frag_tile`: each brick puts at most 4 fragments on one screen tile, and some brick puts exactly 4 there in every draw. `slot_perm`: each row is a permutation of the positions. `tile_owner`: A permutation of the tiles.
All inputs are finite; a program needn't handle non-finite values.
Results may differ from a plain program's by a relative error of at most 0.0035.
Values may be sent and summed in bfloat16 or wider, within the bound.
No kernel may reach another device: no remote copies, remote signals or barrier semaphores. Data moves between devices by JAX's collectives and lax.ppermute only.
A program may use at most 64 MiB of HBM per device.

v0:
```python
import jax
import jax.numpy as jnp
from jax import lax
from jax.sharding import PartitionSpec as P

SAMPLES = 128
RAYS = 256
FRAG = 64
TILE_SIDE = 256
CAP = 4
BLOCK = 16
POS = 16


def in_order(blocks, dim):
    shape = list(blocks.shape[1:])
    shape[dim] *= blocks.shape[0]
    return jnp.moveaxis(blocks, 0, dim).reshape(shape)


def one_gather(arrays, axis, dims):
    vector = jnp.concatenate([a.reshape(-1) for a in arrays])
    lines, at, outs = (lax.all_gather(vector, axis), 0, [])
    for a, dim in zip(arrays, dims):
        blocks = lines[:, at : at + a.size].reshape(-1, *a.shape)
        outs.append(in_order(blocks, dim))
        at += a.size
    return tuple(outs)


def sent_to_all(value, axis):
    copies = jnp.broadcast_to(value, (lax.axis_size(axis), *value.shape))
    return lax.all_to_all(copies, axis, split_axis=0, concat_axis=0, tiled=True)


def collect(value, axis, dim):
    return in_order(sent_to_all(value, axis), dim)


def spline(offset):
    size_abs = jnp.abs(offset)
    inner = 2.0 / 3.0 - size_abs * size_abs + 0.5 * size_abs * size_abs * size_abs
    remain = 2.0 - size_abs
    outer = remain * remain * remain / 6.0
    return jnp.where(size_abs < 1.0, inner, jnp.where(size_abs < 2.0, outer, 0.0))


def tables(shear_pair, sample_index, side, rays, samples):
    cells = jnp.arange(side).astype(jnp.float32)
    depth_pos = (sample_index.astype(jnp.float32) + 0.5) * side / samples - 0.5
    ray_pos = (jnp.arange(rays).astype(jnp.float32) + 0.5) * side / rays - 0.5
    centred = depth_pos - (side - 1) / 2.0
    depth_table = spline(depth_pos[:, None] - cells[None, :])
    row_pos = ray_pos[None, :] + shear_pair[0] * centred[:, None]
    col_pos = ray_pos[None, :] + shear_pair[1] * centred[:, None]
    row_table = spline(row_pos[:, :, None] - cells[None, None, :])
    col_table = spline(col_pos[:, :, None] - cells[None, None, :])
    return (
        depth_table.astype(jnp.bfloat16),
        row_table.astype(jnp.bfloat16),
        col_table.astype(jnp.bfloat16),
    )


def local(
    volume,
    shear,
    absorb,
    color_slope,
    color_bias,
    frag_tile,
    slot_perm,
    frag_rows,
    tile_view,
    tile_owner,
):
    brick = volume[0, 0]
    side = brick.shape[0]
    shear_pair = shear[0, 0]
    rate = absorb[0, 0]
    depth_table, unused_rows, unused_cols = tables(
        shear_pair, jnp.arange(SAMPLES, dtype=jnp.int32), side, 8, SAMPLES
    )
    resampled = jnp.dot(
        depth_table, brick.reshape(side, side * side), preferred_element_type=jnp.float32
    )
    resampled = resampled.astype(jnp.bfloat16).reshape(SAMPLES // BLOCK, BLOCK, side, side)

    def integrate(carry, item):
        optical, colors = carry
        slab_part, block_index = item
        sample_index = block_index * BLOCK + jnp.arange(BLOCK, dtype=jnp.int32)
        unused_depth, row_table, col_table = tables(shear_pair, sample_index, side, RAYS, SAMPLES)
        half_way = jnp.einsum(
            "sua,sab->sub", row_table, slab_part, preferred_element_type=jnp.float32
        ).astype(jnp.bfloat16)
        field = jnp.einsum("sub,svb->suv", half_way, col_table, preferred_element_type=jnp.float32)
        softness = jax.nn.softplus(field)
        before = optical[None] + jnp.cumsum(softness, 0) - softness
        weight = jnp.exp(-rate * before) * (1.0 - jnp.exp(-rate * softness))
        added = jnp.stack(
            [
                jnp.sum(weight * jax.nn.sigmoid(color_slope[k] * field + color_bias[k]), 0)
                for k in range(3)
            ]
        )
        return ((optical + jnp.sum(softness, 0), colors + added), None)

    start = (jnp.zeros((RAYS, RAYS), jnp.float32), jnp.zeros((3, RAYS, RAYS), jnp.float32))
    (optical, colors), unused = lax.scan(
        integrate, start, (resampled, jnp.arange(SAMPLES // BLOCK, dtype=jnp.int32))
    )
    alpha = 1.0 - jnp.exp(-rate * optical)
    image = jnp.concatenate([colors, alpha[None]], 0).astype(jnp.bfloat16)
    per_side = RAYS // FRAG
    count = per_side * per_side
    frags = image.reshape(4, per_side, FRAG, per_side, FRAG).transpose(1, 3, 0, 2, 4)
    keep = (jnp.arange(FRAG)[None, :] < frag_rows[0, 0][:, None]).astype(jnp.bfloat16)
    frags = (frags.reshape(count, 4, FRAG, FRAG) * keep[:, None, :, None]).reshape(
        count, 4 * FRAG * FRAG
    )
    group_size = lax.axis_size("tile")
    column = lax.axis_index("tile")
    target = frag_tile[0, 0, :, 0]
    onehot = (target[:, None] == jnp.arange(group_size)[None, :]).astype(jnp.int32)
    rank = jnp.sum((jnp.cumsum(onehot, 0) - onehot) * onehot, 1)
    row_perm = jnp.sum(onehot[:, :, None] * slot_perm[0, 0][None], 1)
    position = jnp.sum(row_perm * (rank[:, None] == jnp.arange(POS)[None, :]).astype(jnp.int32), 1)
    receiver = jnp.sum(onehot * tile_owner[None, :], 1)
    to_peer = receiver[:, None] == jnp.arange(group_size)[None, :]
    select = to_peer[:, :, None] & (rank[:, None, None] == jnp.arange(CAP)[None, None, :])
    select = select.reshape(count, group_size * CAP).T.astype(jnp.bfloat16)
    outgoing = jnp.dot(select, frags, preferred_element_type=jnp.float32).astype(jnp.bfloat16)
    incoming = lax.all_to_all(
        outgoing.reshape(group_size, CAP, 4 * FRAG * FRAG),
        "tile",
        split_axis=0,
        concat_axis=0,
        tiled=True,
    )
    all_receiver, all_rank, all_position = one_gather((receiver, rank, position), "tile", (0, 0, 0))
    mine = (all_receiver == column).reshape(group_size, count)
    at_place = (
        all_position.reshape(group_size, count)[:, :, None] == jnp.arange(POS)[None, None, :]
    ) & mine[:, :, None]
    at_slot = all_rank.reshape(group_size, count)[:, :, None] == jnp.arange(CAP)[None, None, :]
    place = jnp.einsum("sfp,sfk->psk", at_place.astype(jnp.float32), at_slot.astype(jnp.float32))
    place = place.reshape(POS, group_size * CAP).astype(jnp.bfloat16)
    layer = jnp.dot(
        place,
        incoming.reshape(group_size * CAP, 4 * FRAG * FRAG),
        preferred_element_type=jnp.float32,
    )
    per_tile = TILE_SIDE // FRAG
    tile_image = (
        layer.reshape(per_tile, per_tile, 4, FRAG, FRAG)
        .transpose(2, 0, 3, 1, 4)
        .reshape(4, TILE_SIDE, TILE_SIDE)
    )
    my_view = jnp.sum(jnp.where(tile_owner == column, tile_view, 0))
    slab_count = lax.axis_size("depth")
    strip_rows = TILE_SIDE // slab_count
    stacked = tile_image.reshape(4, slab_count, strip_rows * TILE_SIDE)
    gathered = lax.all_to_all(stacked, "depth", split_axis=1, concat_axis=1, tiled=True)
    ordered = jnp.where(my_view == 1, gathered[:, ::-1], gathered)
    running = jnp.cumprod(1.0 - ordered[3], 0)
    infront = jnp.concatenate([jnp.ones_like(running[:1]), running[:-1]], 0)
    color = jnp.sum(infront[None] * ordered[:3], 1)
    strip = jnp.concatenate([color, 1.0 - running[-1:]], 0).reshape(4, strip_rows, TILE_SIDE)
    finished = collect(strip.astype(jnp.bfloat16), "depth", 1)
    return finished[None]


def solution(mesh):
    in_specs = (
        P("tile", "depth", None, None, None),
        P("tile", "depth", None),
        P("tile", "depth"),
        P(),
        P(),
        P("tile", "depth", None, None),
        P("tile", "depth", None, None),
        P("tile", "depth", None),
        P(),
        P(),
    )
    out_specs = P("tile", None, None, None)
    return jax.shard_map(local, mesh=mesh, in_specs=in_specs, out_specs=out_specs, check_vma=False)
```

profile of v0, /device:TPU:1, one launch (start us, length us, event | category | flops | bytes accessed | tf_op | source)
XLA Modules:
  0.0 338.1 jit_solution(16536058983239158176)
XLA Ops:
  1.6 5.5 %fusion.64 = bf16[16,8,128,128]{3,1,2,0:T(8,128)(2,1)S(1)} fusion(bf16[16,8,128,128]{3,2,1,0:T(8,128)(2,1)} %bitcast.97, f32[128]{0:T(128)S(1)} %iota_convert_fusion.1), kind=kOutput, calls=%fused_computation.69 | convolution fusion | flops 539246592 | bytes 8389120 | tf_op jit(solution)/shard_map/dot_general | solution.py:84
  7.2 3.2 copy.44
  11.0 201.3 %while.18 = (s32[]{:T(128)}, f32[256,256]{1,0:T(8,128)S(1)}, f32[3,256,256]{2,1,0:T(8,128)S(1)}, f32[2]{0:T(128)S(1)}, s32[8]{0:T(128)S(1)}, /*index=5*/bf16[8,1...) while((s32[]{:T(128)}, f32[256,256]{1,0:T(8,128)S(1)}, ...), condition=%wide.region_12.13_spmd.clone, body=%wide.region_6.12_spmd.clone.sunk | while | flops 490874080 | bytes 14225421 | solution.py:110
  14.5 5.5 %fusion.127 = (u16[256,256]{1,0:T(8,128)(2,1)S(1)}, f32[16,256,256]{2,1,0:T(8,128)}) fusion(f32[16,256]{1,0:T(8,128)S(1)} %get-tuple-element.377, f32[128]{0:T(128)S(1)} %iota_convert_fusion.3, f32[16,256]{1,0:T(8,128)S(1)} %get-tuple-element.378, bf16[8,16,128,128]{3,2,1,0:T(8,128)(2,1)} %get-tuple-element.420, s32[]{:T(128)S(6)} %copy.61), kind=kOutput, calls=%fused_computation.33.clone.1 | convolution fusion | flops 426180608 | bytes 4883460 | tf_op jit(solution)/shard_map/while/body/eval_jaxpr/sub,svb->suv/dot_general | solution.py:97
  20.8 15.3 %multiply_reduce_fusion.5 = (f32[256,256]{1,0:T(8,128)S(1)}, f32[256,256]{1,0:T(8,128)S(1)}, f32[256,256]{1,0:T(8,128)S(1)}, f32[256,256]{1,0:T(8,128)S(1)}) fusion(f32[16,256,256]{2,1,0:T(8,128)} %get-tuple-element.379, f32[]{:T(128)} %bitcast.84, f32[]{:T(128)} %bitcast.85, f32[]{:T(128)} %bitcast.86, f32[]{:T(128)} %bitcast.87, f32[]{:T(128)} %bitcast.88, ...), kind=kOutput, calls=%fused_computation.4.clone.1 | output fusion | flops 63700992 | bytes 5636124 | tf_op jit(solution)/shard_map/while/body/eval_jaxpr/jit(cumsum)/reduce_window_sum | solution.py:99
  39.7 5.5 %fusion.127 = (u16[256,256]{1,0:T(8,128)(2,1)S(1)}, f32[16,256,256]{2,1,0:T(8,128)}) fusion(f32[16,256]{1,0:T(8,128)S(1)} %get-tuple-element.377, f32[128]{0:T(128)S(1)} %iota_convert_fusion.3, f32[16,256]{1,0:T(8,128)S(1)} %get-tuple-element.378, bf16[8,16,128,128]{3,2,1,0:T(8,128)(2,1)} %get-tuple-element.420, s32[]{:T(128)S(6)} %copy.61), kind=kOutput, calls=%fused_computation.33.clone.1 | convolution fusion | flops 426180608 | bytes 4883460 | tf_op jit(solution)/shard_map/while/body/eval_jaxpr/sub,svb->suv/dot_general | solution.py:97
  45.9 15.3 %multiply_reduce_fusion.5 = (f32[256,256]{1,0:T(8,128)S(1)}, f32[256,256]{1,0:T(8,128)S(1)}, f32[256,256]{1,0:T(8,128)S(1)}, f32[256,256]{1,0:T(8,128)S(1)}) fusion(f32[16,256,256]{2,1,0:T(8,128)} %get-tuple-element.379, f32[]{:T(128)} %bitcast.84, f32[]{:T(128)} %bitcast.85, f32[]{:T(128)} %bitcast.86, f32[]{:T(128)} %bitcast.87, f32[]{:T(128)} %bitcast.88, ...), kind=kOutput, calls=%fused_computation.4.clone.1 | output fusion | flops 63700992 | bytes 5636124 | tf_op jit(solution)/shard_map/while/body/eval_jaxpr/jit(cumsum)/reduce_window_sum | solution.py:99
  64.8 5.5 %fusion.127 = (u16[256,256]{1,0:T(8,128)(2,1)S(1)}, f32[16,256,256]{2,1,0:T(8,128)}) fusion(f32[16,256]{1,0:T(8,128)S(1)} %get-tuple-element.377, f32[128]{0:T(128)S(1)} %iota_convert_fusion.3, f32[16,256]{1,0:T(8,128)S(1)} %get-tuple-element.378, bf16[8,16,128,128]{3,2,1,0:T(8,128)(2,1)} %get-tuple-element.420, s32[]{:T(128)S(6)} %copy.61), kind=kOutput, calls=%fused_computation.33.clone.1 | convolution fusion | flops 426180608 | bytes 4883460 | tf_op jit(solution)/shard_map/while/body/eval_jaxpr/sub,svb->suv/dot_general | solution.py:97
  71.0 15.3 %multiply_reduce_fusion.5 = (f32[256,256]{1,0:T(8,128)S(1)}, f32[256,256]{1,0:T(8,128)S(1)}, f32[256,256]{1,0:T(8,128)S(1)}, f32[256,256]{1,0:T(8,128)S(1)}) fusion(f32[16,256,256]{2,1,0:T(8,128)} %get-tuple-element.379, f32[]{:T(128)} %bitcast.84, f32[]{:T(128)} %bitcast.85, f32[]{:T(128)} %bitcast.86, f32[]{:T(128)} %bitcast.87, f32[]{:T(128)} %bitcast.88, ...), kind=kOutput, calls=%fused_computation.4.clone.1 | output fusion | flops 63700992 | bytes 5636124 | tf_op jit(solution)/shard_map/while/body/eval_jaxpr/jit(cumsum)/reduce_window_sum | solution.py:99
  88.6 1.2 fusion.126
  89.9 5.5 %fusion.127 = (u16[256,256]{1,0:T(8,128)(2,1)S(1)}, f32[16,256,256]{2,1,0:T(8,128)}) fusion(f32[16,256]{1,0:T(8,128)S(1)} %get-tuple-element.377, f32[128]{0:T(128)S(1)} %iota_convert_fusion.3, f32[16,256]{1,0:T(8,128)S(1)} %get-tuple-element.378, bf16[8,16,128,128]{3,2,1,0:T(8,128)(2,1)} %get-tuple-element.420, s32[]{:T(128)S(6)} %copy.61), kind=kOutput, calls=%fused_computation.33.clone.1 | convolution fusion | flops 426180608 | bytes 4883460 | tf_op jit(solution)/shard_map/while/body/eval_jaxpr/sub,svb->suv/dot_general | solution.py:97
  96.2 15.3 %multiply_reduce_fusion.5 = (f32[256,256]{1,0:T(8,128)S(1)}, f32[256,256]{1,0:T(8,128)S(1)}, f32[256,256]{1,0:T(8,128)S(1)}, f32[256,256]{1,0:T(8,128)S(1)}) fusion(f32[16,256,256]{2,1,0:T(8,128)} %get-tuple-element.379, f32[]{:T(128)} %bitcast.84, f32[]{:T(128)} %bitcast.85, f32[]{:T(128)} %bitcast.86, f32[]{:T(128)} %bitcast.87, f32[]{:T(128)} %bitcast.88, ...), kind=kOutput, calls=%fused_computation.4.clone.1 | output fusion | flops 63700992 | bytes 5636124 | tf_op jit(solution)/shard_map/while/body/eval_jaxpr/jit(cumsum)/reduce_window_sum | solution.py:99
  115.1 5.5 %fusion.127 = (u16[256,256]{1,0:T(8,128)(2,1)S(1)}, f32[16,256,256]{2,1,0:T(8,128)}) fusion(f32[16,256]{1,0:T(8,128)S(1)} %get-tuple-element.377, f32[128]{0:T(128)S(1)} %iota_convert_fusion.3, f32[16,256]{1,0:T(8,128)S(1)} %get-tuple-element.378, bf16[8,16,128,128]{3,2,1,0:T(8,128)(2,1)} %get-tuple-element.420, s32[]{:T(128)S(6)} %copy.61), kind=kOutput, calls=%fused_computation.33.clone.1 | convolution fusion | flops 426180608 | bytes 4883460 | tf_op jit(solution)/shard_map/while/body/eval_jaxpr/sub,svb->suv/dot_general | solution.py:97
  121.3 15.3 %multiply_reduce_fusion.5 = (f32[256,256]{1,0:T(8,128)S(1)}, f32[256,256]{1,0:T(8,128)S(1)}, f32[256,256]{1,0:T(8,128)S(1)}, f32[256,256]{1,0:T(8,128)S(1)}) fusion(f32[16,256,256]{2,1,0:T(8,128)} %get-tuple-element.379, f32[]{:T(128)} %bitcast.84, f32[]{:T(128)} %bitcast.85, f32[]{:T(128)} %bitcast.86, f32[]{:T(128)} %bitcast.87, f32[]{:T(128)} %bitcast.88, ...), kind=kOutput, calls=%fused_computation.4.clone.1 | output fusion | flops 63700992 | bytes 5636124 | tf_op jit(solution)/shard_map/while/body/eval_jaxpr/jit(cumsum)/reduce_window_sum | solution.py:99
  140.2 5.5 %fusion.127 = (u16[256,256]{1,0:T(8,128)(2,1)S(1)}, f32[16,256,256]{2,1,0:T(8,128)}) fusion(f32[16,256]{1,0:T(8,128)S(1)} %get-tuple-element.377, f32[128]{0:T(128)S(1)} %iota_convert_fusion.3, f32[16,256]{1,0:T(8,128)S(1)} %get-tuple-element.378, bf16[8,16,128,128]{3,2,1,0:T(8,128)(2,1)} %get-tuple-element.420, s32[]{:T(128)S(6)} %copy.61), kind=kOutput, calls=%fused_computation.33.clone.1 | convolution fusion | flops 426180608 | bytes 4883460 | tf_op jit(solution)/shard_map/while/body/eval_jaxpr/sub,svb->suv/dot_general | solution.py:97
  146.5 15.3 %multiply_reduce_fusion.5 = (f32[256,256]{1,0:T(8,128)S(1)}, f32[256,256]{1,0:T(8,128)S(1)}, f32[256,256]{1,0:T(8,128)S(1)}, f32[256,256]{1,0:T(8,128)S(1)}) fusion(f32[16,256,256]{2,1,0:T(8,128)} %get-tuple-element.379, f32[]{:T(128)} %bitcast.84, f32[]{:T(128)} %bitcast.85, f32[]{:T(128)} %bitcast.86, f32[]{:T(128)} %bitcast.87, f32[]{:T(128)} %bitcast.88, ...), kind=kOutput, calls=%fused_computation.4.clone.1 | output fusion | flops 63700992 | bytes 5636124 | tf_op jit(solution)/shard_map/while/body/eval_jaxpr/jit(cumsum)/reduce_window_sum | solution.py:99
  165.4 5.5 %fusion.127 = (u16[256,256]{1,0:T(8,128)(2,1)S(1)}, f32[16,256,256]{2,1,0:T(8,128)}) fusion(f32[16,256]{1,0:T(8,128)S(1)} %get-tuple-element.377, f32[128]{0:T(128)S(1)} %iota_convert_fusion.3, f32[16,256]{1,0:T(8,128)S(1)} %get-tuple-element.378, bf16[8,16,128,128]{3,2,1,0:T(8,128)(2,1)} %get-tuple-element.420, s32[]{:T(128)S(6)} %copy.61), kind=kOutput, calls=%fused_computation.33.clone.1 | convolution fusion | flops 426180608 | bytes 4883460 | tf_op jit(solution)/shard_map/while/body/eval_jaxpr/sub,svb->suv/dot_general | solution.py:97
  171.6 15.3 %multiply_reduce_fusion.5 = (f32[256,256]{1,0:T(8,128)S(1)}, f32[256,256]{1,0:T(8,128)S(1)}, f32[256,256]{1,0:T(8,128)S(1)}, f32[256,256]{1,0:T(8,128)S(1)}) fusion(f32[16,256,256]{2,1,0:T(8,128)} %get-tuple-element.379, f32[]{:T(128)} %bitcast.84, f32[]{:T(128)} %bitcast.85, f32[]{:T(128)} %bitcast.86, f32[]{:T(128)} %bitcast.87, f32[]{:T(128)} %bitcast.88, ...), kind=kOutput, calls=%fused_computation.4.clone.1 | output fusion | flops 63700992 | bytes 5636124 | tf_op jit(solution)/shard_map/while/body/eval_jaxpr/jit(cumsum)/reduce_window_sum | solution.py:99
  189.2 1.2 fusion.126
  190.5 5.5 %fusion.127 = (u16[256,256]{1,0:T(8,128)(2,1)S(1)}, f32[16,256,256]{2,1,0:T(8,128)}) fusion(f32[16,256]{1,0:T(8,128)S(1)} %get-tuple-element.377, f32[128]{0:T(128)S(1)} %iota_convert_fusion.3, f32[16,256]{1,0:T(8,128)S(1)} %get-tuple-element.378, bf16[8,16,128,128]{3,2,1,0:T(8,128)(2,1)} %get-tuple-element.420, s32[]{:T(128)S(6)} %copy.61), kind=kOutput, calls=%fused_computation.33.clone.1 | convolution fusion | flops 426180608 | bytes 4883460 | tf_op jit(solution)/shard_map/while/body/eval_jaxpr/sub,svb->suv/dot_general | solution.py:97
  196.8 15.3 %multiply_reduce_fusion.5 = (f32[256,256]{1,0:T(8,128)S(1)}, f32[256,256]{1,0:T(8,128)S(1)}, f32[256,256]{1,0:T(8,128)S(1)}, f32[256,256]{1,0:T(8,128)S(1)}) fusion(f32[16,256,256]{2,1,0:T(8,128)} %get-tuple-element.379, f32[]{:T(128)} %bitcast.84, f32[]{:T(128)} %bitcast.85, f32[]{:T(128)} %bitcast.86, f32[]{:T(128)} %bitcast.87, f32[]{:T(128)} %bitcast.88, ...), kind=kOutput, calls=%fused_computation.4.clone.1 | output fusion | flops 63700992 | bytes 5636124 | tf_op jit(solution)/shard_map/while/body/eval_jaxpr/jit(cumsum)/reduce_window_sum | solution.py:99
  216.4 2.2 reshape.245
  218.6 7.6 %all-to-all-start = ((bf16[16,4,16384]{2,1,0:T(4,128)(2,1)}), bf16[16,4,16384]{2,1,0:T(4,128)(2,1)}, u32[]{:S(2)}, u32[]{:S(2)}) async-start(bf16[16,4,16384]{2,1,0:T(4,128)(2,1)} %reshape.245), calls=%async_computation | async-start | bytes 4194304 | tf_op jit(solution)/shard_map/all_to_all | solution.py:134
  228.0 28.3 %all-reduce.1 = s32[768]{0:T(1024)S(1)} all-reduce(s32[768]{0:T(1024)S(1)} %add_dynamic-update-slice_fusion), channel_id=2, replica_groups=mesh['tile'=16,'depth'=16] {'tile'}, use_global_device_ids=true, to_apply=%add.1 | all-reduce | flops 768 | bytes 6144
  256.9 2.8 reshape.246
  259.6 3.2 copy.34
  262.8 8.9 %convolution_bitcast_fusion = f32[4,4,64,4,64]{4,3,2,0,1:T(4,128)S(1)} fusion(bf16[4,64,64,64,1]{3,2,1,0,4:T(8,128)(2,1)} %bitcast.96, bf16[4,4,64,1,1]{1,0,2,4,3:T(4,128)(2,1)S(1)} %bitcast.103), kind=kOutput, calls=%fused_computation.70 | convolution fusion | flops 33554432 | bytes 3147776 | tf_op jit(solution)/shard_map/dot_general | solution.py:149
  272.0 1.5 reshape_reshape.3
  273.5 1.7 copy.36
  275.2 12.2 %all-to-all-start.1 = ((f32[4,16,4096]{2,0,1:T(4,128)}), f32[4,16,4096]{2,0,1:T(4,128)S(1)}, u32[]{:S(2)}, u32[]{:S(2)}) async-start(f32[4,16,4096]{2,0,1:T(4,128)} %copy.36), calls=%async_computation.1 | async-start | bytes 2097152 | tf_op jit(solution)/shard_map/all_to_all | solution.py:164
  288.7 26.7 %all-to-all-done.1 = f32[4,16,4096]{2,0,1:T(4,128)S(1)} async-done(((f32[4,16,4096]{2,0,1:T(4,128)}), f32[4,16,4096]{2,0,1:T(4,128)S(1)}, u32[]{:S(2)}, u32[]{:S(2)}) %all-to-all-start.1) | async-done | bytes 1048608 | tf_op jit(solution)/shard_map/all_to_all | solution.py:164
  316.8 20.4 %all_to_all.15 = bf16[16,4,16,256]{3,2,1,0:T(8,128)(2,1)S(1)} all-to-all(bf16[16,4,16,256]{3,2,1,0:T(8,128)(2,1)S(1)} %broadcast_in_dim.38), channel_id=1, replica_groups=mesh['tile'=16,'depth'=16] {'depth'}, dimensions={0} | all-to-all | bytes 1048576 | tf_op jit(solution)/shard_map/all_to_all | solution.py:33
  (141 shorter events, 36.4 us)
Async XLA Ops:
  7.1 3.9 %copy-start = (f32[3]{0:T(128)S(1)}, f32[3]{0:T(128)}, u32[]{:S(2)}) copy-start(f32[3]{0:T(128)} %param.15) | copy-start | bytes 40
  7.1 3.9 %copy-start.1 = (f32[3]{0:T(128)S(1)}, f32[3]{0:T(128)}, u32[]{:S(2)}) copy-start(f32[3]{0:T(128)} %param.16) | copy-start | bytes 40
  7.2 3.9 %copy-start.2 = (f32[1,1,2]{2,1,0:T(1,128)S(1)}, f32[1,1,2]{2,1,0:T(1,128)}, u32[]{:S(2)}) copy-start(f32[1,1,2]{2,1,0:T(1,128)} %param.13) | copy-start | bytes 28
  212.4 1.4 copy-start.6
  216.4 9.9 %copy-start.7 = (u32[256]{0:T(256)S(1)}, u32[256]{0:T(256)}, u32[]{:S(2)}) copy-start(u32[256]{0:T(256)} %constant.180) | copy-start | bytes 3076
  216.4 11.1 %copy-start.3 = (s32[1,1,16,16]{3,2,1,0:T(8,128)S(1)}, s32[1,1,16,16]{3,2,1,0:T(8,128)}, u32[]{:S(2)}) copy-start(s32[1,1,16,16]{3,2,1,0:T(8,128)} %param.18) | copy-start | bytes 3076
  218.6 38.2 %all-to-all-start = ((bf16[16,4,16384]{2,1,0:T(4,128)(2,1)}), bf16[16,4,16384]{2,1,0:T(4,128)(2,1)}, u32[]{:S(2)}, u32[]{:S(2)}) async-start(bf16[16,4,16384]{2,1,0:T(4,128)(2,1)} %reshape.245), calls=%async_computation | async-start | bytes 4194304 | tf_op jit(solution)/shard_map/all_to_all | solution.py:134
  272.0 15.4 %copy-start.4 = (s32[16]{0:T(128)S(1)}, s32[16]{0:T(128)}, u32[]{:S(2)}) copy-start(s32[16]{0:T(128)} %param.21) | copy-start | bytes 196
  272.0 15.4 %copy-start.5 = (s32[16]{0:T(128)S(1)}, s32[16]{0:T(128)}, u32[]{:S(2)}) copy-start(s32[16]{0:T(128)} %param.20) | copy-start | bytes 196
  275.2 40.2 %all-to-all-start.1 = ((f32[4,16,4096]{2,0,1:T(4,128)}), f32[4,16,4096]{2,0,1:T(4,128)S(1)}, u32[]{:S(2)}, u32[]{:S(2)}) async-start(f32[4,16,4096]{2,0,1:T(4,128)} %copy.36), calls=%async_computation.1 | async-start | bytes 2097152 | tf_op jit(solution)/shard_map/all_to_all | solution.py:164
where the time goes:
time: 340 us; the launch traced here: 338 us
  other arithmetic  140 us (41%)
  matrix products  59.7 us (18%)
  blocking collectives  48.8 us (14%)
  local copies, waits for them, and re-layouts  34.3 us (10%)
  waiting for transfers between devices  26.7 us (8%)
  starting transfers between devices  19.8 us (6%)
  loops' own time  6.22 us (2%)
    another operation x8, other arithmetic, integrate(): before = optical[None] + jnp.cumsum(softness, 0) - softness  122 us
    dot_general x8, matrix products, integrate(): jnp.einsum('sub,svb->suv', half_way, col_table, preferred_element_type=jn...  44.3 us
    unnamed x1, blocking collectives  28.3 us
    all_to_all x1, waiting for transfers between devices, local(): lax.all_to_all(stacked, 'depth', split_axis=1, concat_axis=1, tiled=True)  26.7 us
    all_to_all x1, blocking collectives, sent_to_all(): return lax.all_to_all(copies, axis, split_axis=0, concat_axis=0, tiled=True)  20.4 us
    all_to_all x1, starting transfers between devices, local(): lax.all_to_all(stacked, 'depth', split_axis=1, concat_axis=1, tiled=True)  12.2 us
    mul x8, other arithmetic, tables(): col_pos = ray_pos[None, :] + shear_pair[1] * centred[:, None]  9.82 us
    dot_general x1, matrix products, local(): jnp.dot(place, incoming.reshape(group_size * CAP, 4 * FRAG * FRAG), prefe...  8.93 us
  transfers between devices with their start and end apart: 2, of which 1 were waited for; matrix products, arithmetic and copies ran while one was open for 1% of the time, Pallas kernels for 0%

commit v1 on v0

--- a/solution.py
+++ b/solution.py
@@ -1,14 +1,21 @@
+import math
 import jax
 import jax.numpy as jnp
+import numpy as np
 from jax import lax
+from jax.experimental import pallas as pl
+from jax.experimental.pallas import tpu as pltpu
 from jax.sharding import PartitionSpec as P
 
 SAMPLES = 128
 RAYS = 256
+SIDE = 128
+STEP = 8
+ROWS = RAYS // STEP
+LOG2E = math.log2(math.e)
 FRAG = 64
 TILE_SIDE = 256
 CAP = 4
-BLOCK = 16
 POS = 16
 
 
@@ -45,21 +52,138 @@
     return jnp.where(size_abs < 1.0, inner, jnp.where(size_abs < 2.0, outer, 0.0))
 
 
-def tables(shear_pair, sample_index, side, rays, samples):
-    cells = jnp.arange(side).astype(jnp.float32)
-    depth_pos = (sample_index.astype(jnp.float32) + 0.5) * side / samples - 0.5
-    ray_pos = (jnp.arange(rays).astype(jnp.float32) + 0.5) * side / rays - 0.5
-    centred = depth_pos - (side - 1) / 2.0
-    depth_table = spline(depth_pos[:, None] - cells[None, :])
-    row_pos = ray_pos[None, :] + shear_pair[0] * centred[:, None]
-    col_pos = ray_pos[None, :] + shear_pair[1] * centred[:, None]
-    row_table = spline(row_pos[:, :, None] - cells[None, None, :])
-    col_table = spline(col_pos[:, :, None] - cells[None, None, :])
-    return (
-        depth_table.astype(jnp.bfloat16),
-        row_table.astype(jnp.bfloat16),
-        col_table.astype(jnp.bfloat16),
-    )
+def wrapped(diff):
+    return jnp.bitwise_and(diff + 64, 127) - 64
+
+
+def band(base, mask_ref):
+    parts = []
+    for k in range(SIDE // 16):
+        part = pltpu.roll(base, 16 * k, 1) if k else base
+        if k not in (3, 4):
+            part = part * mask_ref[pl.ds(16 * k, 16), :]
+        parts.append(part)
+    return jnp.concatenate(parts, 0)
+
+
+def render_kernel(par_ref, prev_ref, vol_ref, next_ref, out_ref, field_ref, cum_ref, clear_ref, acc_ref, mask_ref):
+    step = pl.program_id(0)
+    steps = SAMPLES // STEP
+    slot = lax.rem(step, 2)
+    w0 = float(np.float32(2.0 / 3.0).astype(jnp.bfloat16))
+    w1 = float(np.float32(1.0 / 6.0).astype(jnp.bfloat16))
+
+    @pl.when(step == 0)
+    def _():
+        r = lax.broadcasted_iota(jnp.int32, (SIDE, SIDE), 0)
+        c = lax.broadcasted_iota(jnp.int32, (SIDE, SIDE), 1)
+        mask_ref[...] = jnp.where(jnp.abs(r - c) < 64, 1.0, 0.0).astype(jnp.bfloat16)
+        cum_ref[...] = jnp.zeros_like(cum_ref)
+        clear_ref[...] = jnp.ones_like(clear_ref)
+        acc_ref[...] = jnp.zeros_like(acc_ref)
+
+    def make_field(j):
+        s = step * STEP + j
+        centred = s.astype(jnp.float32) - (SIDE - 1) / 2.0
+        lo = jnp.maximum(j - 1, 0)
+        hi = jnp.minimum(j + 1, STEP - 1)
+        before = jnp.where(j == 0, prev_ref[0], vol_ref[lo]).astype(jnp.float32)
+        after = jnp.where(j == STEP - 1, next_ref[0], vol_ref[hi]).astype(jnp.float32)
+        wb = jnp.where(s == 0, 0.0, w1)
+        wa = jnp.where(s == SAMPLES - 1, 0.0, w1)
+        cells = (w0 * vol_ref[j].astype(jnp.float32) + (wb * before + wa * after)).astype(jnp.bfloat16)
+        i = lax.broadcasted_iota(jnp.int32, (16, SIDE), 0)
+        a = lax.broadcasted_iota(jnp.int32, (16, SIDE), 1)
+        d_row = wrapped(i - a).astype(jnp.float32)
+        d_col = wrapped(a - i).astype(jnp.float32)
+        shift_r = par_ref[0] * centred
+        shift_c = par_ref[1] * centred
+        rows = jnp.concatenate(
+            [band(spline(d_row + (shift_r + q)).astype(jnp.bfloat16), mask_ref) for q in (-0.25, 0.25)], 0
+        )
+        cols = jnp.concatenate(
+            [band(spline(d_col + (shift_c + q)).astype(jnp.bfloat16), mask_ref) for q in (-0.25, 0.25)], 1
+        )
+        half = jnp.dot(rows, cells, preferred_element_type=jnp.float32).astype(jnp.bfloat16)
+        field_ref[slot, j] = jnp.dot(half, cols, preferred_element_type=jnp.float32)
+
+    def integrate(r):
+        neg_rate = par_ref[2]
+        for sub in range(ROWS // 8):
+            at = pl.ds(pl.multiple_of(r * ROWS + 8 * sub, 8), 8)
+            cum = cum_ref[at, :]
+            clear = clear_ref[at, :]
+            acc = [acc_ref[k, at, :] for k in range(3)]
+            for j in range(STEP):
+                f = field_ref[1 - slot, j, at, :]
+                cum = cum + jnp.log(1.0 + jnp.exp2(f * LOG2E))
+                after = jnp.exp2(neg_rate * cum)
+                w = clear - after
+                clear = after
+                for k in range(3):
+                    acc[k] = acc[k] + w * jnp.tanh(f * par_ref[3 + k] + par_ref[6 + k])
+            cum_ref[at, :] = cum
+            clear_ref[at, :] = clear
+            for k in range(3):
+                acc_ref[k, at, :] = acc[k]
+
+    @pl.when(step == 0)
+    def _():
+        @pl.loop(0, STEP)
+        def _(r):
+            make_field(r)
+
+    @pl.when((step > 0) & (step < steps))
+    def _():
+        @pl.loop(0, STEP)
+        def _(r):
+            make_field(r)
+            integrate(r)
+
+    @pl.when(step == steps)
+    def _():
+        @pl.loop(0, STEP)
+        def _(r):
+            integrate(r)
+
+        r = lax.broadcasted_iota(jnp.int32, (RAYS, RAYS), 0)
+        c = lax.broadcasted_iota(jnp.int32, (RAYS, RAYS), 1)
+        half = RAYS // 2
+        left = (c == jnp.bitwise_and(r, 1) * half + jnp.right_shift(r, 1)).astype(jnp.float32).astype(jnp.bfloat16)
+        right = (r == jnp.bitwise_and(c, 1) * half + jnp.right_shift(c, 1)).astype(jnp.float32).astype(jnp.bfloat16)
+        alpha = 1.0 - clear_ref[...]
+        for k in range(4):
+            plane = alpha if k == 3 else 0.5 * (alpha + acc_ref[k])
+            plane = jnp.dot(left, plane.astype(jnp.bfloat16), preferred_element_type=jnp.float32)
+            plane = jnp.dot(plane.astype(jnp.bfloat16), right, preferred_element_type=jnp.float32)
+            out_ref[k] = plane.astype(jnp.bfloat16)
+
+
+def render(brick, shear_pair, rate, slope, bias):
+    params = jnp.concatenate([shear_pair, -LOG2E * rate[None], 0.5 * slope, 0.5 * bias])
+    steps = SAMPLES // STEP
+    at = lambda i: jnp.minimum(i, steps - 1)
+    return pl.pallas_call(
+        render_kernel,
+        grid=(steps + 1,),
+        in_specs=[
+            pl.BlockSpec(memory_space=pltpu.SMEM),
+            pl.BlockSpec((1, SIDE, SIDE), lambda i: (jnp.maximum(at(i) * STEP - 1, 0), 0, 0)),
+            pl.BlockSpec((STEP, SIDE, SIDE), lambda i: (at(i), 0, 0)),
+            pl.BlockSpec((1, SIDE, SIDE), lambda i: (jnp.minimum(at(i) * STEP + STEP, SAMPLES - 1), 0, 0)),
+        ],
+        out_specs=pl.BlockSpec((4, RAYS, RAYS), lambda i: (0, 0, 0)),
+        out_shape=jax.ShapeDtypeStruct((4, RAYS, RAYS), jnp.bfloat16),
+        scratch_shapes=[
+            pltpu.VMEM((2, STEP, RAYS, RAYS), jnp.float32),
+            pltpu.VMEM((RAYS, RAYS), jnp.float32),
+            pltpu.VMEM((RAYS, RAYS), jnp.float32),
+            pltpu.VMEM((3, RAYS, RAYS), jnp.float32),
+            pltpu.VMEM((SIDE, SIDE), jnp.bfloat16),
+        ],
+        compiler_params=pltpu.CompilerParams(dimension_semantics=("arbitrary",), vmem_limit_bytes=32 * 2**20),
+        name="render",
+    )(params, brick, brick, brick)
 
 
 def local(
@@ -75,43 +199,7 @@
     tile_owner,
 ):
     brick = volume[0, 0]
-    side = brick.shape[0]
-    shear_pair = shear[0, 0]
-    rate = absorb[0, 0]
-    depth_table, unused_rows, unused_cols = tables(
-        shear_pair, jnp.arange(SAMPLES, dtype=jnp.int32), side, 8, SAMPLES
-    )
-    resampled = jnp.dot(
-        depth_table, brick.reshape(side, side * side), preferred_element_type=jnp.float32
-    )
-    resampled = resampled.astype(jnp.bfloat16).reshape(SAMPLES // BLOCK, BLOCK, side, side)
-
-    def integrate(carry, item):
-        optical, colors = carry
-        slab_part, block_index = item
-        sample_index = block_index * BLOCK + jnp.arange(BLOCK, dtype=jnp.int32)
-        unused_depth, row_table, col_table = tables(shear_pair, sample_index, side, RAYS, SAMPLES)
-        half_way = jnp.einsum(
-            "sua,sab->sub", row_table, slab_part, preferred_element_type=jnp.float32
-        ).astype(jnp.bfloat16)
-        field = jnp.einsum("sub,svb->suv", half_way, col_table, preferred_element_type=jnp.float32)
-        softness = jax.nn.softplus(field)
-        before = optical[None] + jnp.cumsum(softness, 0) - softness
-        weight = jnp.exp(-rate * before) * (1.0 - jnp.exp(-rate * softness))
-        added = jnp.stack(
-            [
-                jnp.sum(weight * jax.nn.sigmoid(color_slope[k] * field + color_bias[k]), 0)
-                for k in range(3)
-            ]
-        )
-        return ((optical + jnp.sum(softness, 0), colors + added), None)
-
-    start = (jnp.zeros((RAYS, RAYS), jnp.float32), jnp.zeros((3, RAYS, RAYS), jnp.float32))
-    (optical, colors), unused = lax.scan(
-        integrate, start, (resampled, jnp.arange(SAMPLES // BLOCK, dtype=jnp.int32))
-    )
-    alpha = 1.0 - jnp.exp(-rate * optical)
-    image = jnp.concatenate([colors, alpha[None]], 0).astype(jnp.bfloat16)
+    image = render(brick, shear[0, 0], absorb[0, 0], color_slope, color_bias)
     per_side = RAYS // FRAG
     count = per_side * per_side
     frags = image.reshape(4, per_side, FRAG, per_side, FRAG).transpose(1, 3, 0, 2, 4)

time: 340 us -> 214 us (0.63)
  other arithmetic: 140 us -> 6.93 us
  Pallas kernels: 0 us -> 80.5 us
  matrix products: 59.7 us -> 9.86 us
  local copies, waits for them, and re-layouts: 34.3 us -> 17.3 us
  loops' own time: 6.22 us -> 0 us
    another operation x11 -> x1, other arithmetic: 122 us -> 0.02 us  [the longest x8 122 us: integrate(): before = optical[None] + jnp.cumsum(softness, 0) - softness]
    pallas_call x0 -> x1, Pallas kernels: none -> 80.5 us  [render(): pl.pallas_call(render_kernel, grid=(steps + 1,), in_specs=[pl.BlockSpec(m...]
    dot_general x9 -> x0, matrix products: 49.8 us -> none  [the longest x8 44.3 us: integrate(): jnp.einsum('sub,svb->suv', half_way, col_table, preferred_element_type=jn...]
    slice x16 -> x0, local copies, waits for them, and re-layouts: 10.2 us -> none  [the longest x8 5.28 us: integrate(): color_slope[k] * field + color_bias[k]]
    mul x8 -> x1, other arithmetic: 9.82 us -> 0.68 us  [render(): 0.5 * bias]
    another operation x1 -> x0, loops' own time: 6.22 us -> none  [local(): lax.scan(integrate, start, (resampled, jnp.arange(SAMPLES // BLOCK, dtype...]
    dynamic_slice x8 -> x0, local copies, waits for them, and re-layouts: 5.28 us -> none  [local(): lax.scan(integrate, start, (resampled, jnp.arange(SAMPLES // BLOCK, dtype...]
where the time goes in v1:
time: 214 us; the launch traced here: 212 us
  Pallas kernels  80.5 us (38%)
  blocking collectives  48.8 us (23%)
  waiting for transfers between devices  26.7 us (12%)
  starting transfers between devices  20 us (9%)
  local copies, waits for them, and re-layouts  17.3 us (8%)
  matrix products  9.86 us (5%)
  other arithmetic  6.93 us (3%)
  between operations  2.17 us (1%)
    pallas_call x1, Pallas kernels, render(): pl.pallas_call(render_kernel, grid=(steps + 1,), in_specs=[pl.BlockSpec(m...  80.5 us
    unnamed x1, blocking collectives  28.3 us
    all_to_all x1, waiting for transfers between devices, local(): lax.all_to_all(stacked, 'depth', split_axis=1, concat_axis=1, tiled=True)  26.7 us
    all_to_all x1, blocking collectives, sent_to_all(): return lax.all_to_all(copies, axis, split_axis=0, concat_axis=0, tiled=True)  20.4 us
    all_to_all x1, starting transfers between devices, local(): lax.all_to_all(stacked, 'depth', split_axis=1, concat_axis=1, tiled=True)  12.2 us
    dot_general x1, matrix products, local(): jnp.dot(place, incoming.reshape(group_size * CAP, 4 * FRAG * FRAG), prefe...  8.93 us
    all_to_all x1, starting transfers between devices, local(): lax.all_to_all(outgoing.reshape(group_size, CAP, 4 * FRAG * FRAG), 'tile'...  7.76 us
    reshape x2, local copies, waits for them, and re-layouts, local(): incoming.reshape(group_size * CAP, 4 * FRAG * FRAG)  5.74 us
  transfers between devices with their start and end apart: 2, of which 1 were waited for; matrix products, arithmetic and copies ran while one was open for 1% of the time, Pallas kernels for 0%

profile of v1, /device:TPU:1, one launch (start us, length us, event | category | flops | bytes accessed | tf_op | source)
XLA Modules:
  0.0 212.2 jit_solution(16368481650354819438)
XLA Ops:
  0.7 0.5 broadcast.94
  1.2 1.3 reduce.3
  2.6 0.7 fusion.9
  3.4 0.9 select_reduce_fusion.2
  4.3 0.7 broadcast_multiply_fusion
  5.0 0.7 pad_maximum_fusion.1.par_ref
  5.7 2.2 %copy-done = bf16[1,1,128,128,128]{4,3,2,1,0:T(8,128)(2,1)S(1)} copy-done((bf16[1,1,128,128,128]{4,3,2,1,0:T(8,128)(2,1)S(1)}, bf16[1,1,128,128,128]{4,3,2,1,0:T(8,128)(2,1)}, u32[]{:S(2)}) %copy-start) | copy-done | bytes 4194328
  7.9 80.5 %render.1 = bf16[4,256,256]{2,1,0:T(8,128)(2,1)S(1)} custom-call(f32[9]{0:T(128)S(1)} %pad_maximum_fusion.1.par_ref, bf16[128,128,128]{2,1,0:T(8,128)(2,1)S(1)} %bitcast.37, bf16[128,128,128]{2,1,0:T(8,128)(2,1)S(1)} %bitcast.38, bf16[128,128,128]{2,1,0:T(8,128)(2,1)S(1)} %bitcast.39), custom_call_target="tpu_custom_call" | custom-call | tf_op jit(solution)/shard_map/render/pallas_call | solution.py:166
  88.4 0.4 reshape.140
  88.8 0.2 bitcast_multiply_fusion
  89.0 0.8 mul.77
  89.9 0.7 convolution_convert_fusion
  90.6 2.2 %reshape.141 = bf16[16,4,16384]{2,1,0:T(4,128)(2,1)} reshape(bf16[64,16384]{1,0:T(8,128)(2,1)S(1)} %convolution_convert_fusion) | data formatting | bytes 4194304 | tf_op jit(solution)/shard_map/reshape | solution.py:223
  92.8 7.8 %all-to-all-start = ((bf16[16,4,16384]{2,1,0:T(4,128)(2,1)}), bf16[16,4,16384]{2,1,0:T(4,128)(2,1)}, u32[]{:S(2)}, u32[]{:S(2)}) async-start(bf16[16,4,16384]{2,1,0:T(4,128)(2,1)} %reshape.141), calls=%async_computation | async-start | bytes 4194304 | tf_op jit(solution)/shard_map/all_to_all | solution.py:222
  100.6 0.6 dynamic-slice
  102.3 28.3 %all-reduce.1 = s32[768]{0:T(1024)S(1)} all-reduce(s32[768]{0:T(1024)S(1)} %add_dynamic-update-slice_fusion), channel_id=2, replica_groups=mesh['tile'=16,'depth'=16] {'tile'}, use_global_device_ids=true, to_apply=%add.1 | all-reduce | flops 768 | bytes 6144
  130.8 0.3 fusion
  131.2 2.6 %reshape.142 = bf16[64,16384]{1,0:T(8,128)(2,1)S(1)} reshape(bf16[16,4,16384]{2,1,0:T(4,128)(2,1)} %all-to-all-done) | data formatting | bytes 4194304 | tf_op jit(solution)/shard_map/reshape | solution.py:239
  133.7 3.2 %copy.30 = bf16[64,16384]{0,1:T(8,128)(2,1)} copy(bf16[64,16384]{1,0:T(8,128)(2,1)S(1)} %reshape.142) | data formatting | bytes 4194304 | tf_op jit(solution)/shard_map/reshape | solution.py:239
  136.9 8.9 %convolution_bitcast_fusion = f32[4,4,64,4,64]{4,3,2,0,1:T(4,128)S(1)} fusion(bf16[4,64,64,64,1]{3,2,1,0,4:T(8,128)(2,1)} %bitcast.40, bf16[4,4,64,1,1]{1,0,2,4,3:T(4,128)(2,1)S(1)} %bitcast.45), kind=kOutput, calls=%fused_computation.1 | convolution fusion | flops 33554432 | bytes 3147776 | tf_op jit(solution)/shard_map/dot_general | solution.py:237
  145.8 0.2 copy.31
  146.1 1.5 reshape_reshape.3
  147.6 1.7 copy.32
  149.2 12.2 %all-to-all-start.1 = ((f32[4,16,4096]{2,0,1:T(4,128)}), f32[4,16,4096]{2,0,1:T(4,128)S(1)}, u32[]{:S(2)}, u32[]{:S(2)}) async-start(f32[4,16,4096]{2,0,1:T(4,128)} %copy.32), calls=%async_computation.1 | async-start | bytes 2097152 | tf_op jit(solution)/shard_map/all_to_all | solution.py:252
  161.5 0.6 fusion.11
  162.8 26.7 %all-to-all-done.1 = f32[4,16,4096]{2,0,1:T(4,128)S(1)} async-done(((f32[4,16,4096]{2,0,1:T(4,128)}), f32[4,16,4096]{2,0,1:T(4,128)S(1)}, u32[]{:S(2)}, u32[]{:S(2)}) %all-to-all-start.1) | async-done | bytes 1048608 | tf_op jit(solution)/shard_map/all_to_all | solution.py:252
  189.4 0.2 reverse_select_fusion
  189.7 0.3 slice_subtract_fusion
  190.2 0.2 reduce_window.9
  190.5 0.3 fusion.1
  190.9 20.4 %all_to_all.15 = bf16[16,4,16,256]{3,2,1,0:T(8,128)(2,1)S(1)} all-to-all(bf16[16,4,16,256]{3,2,1,0:T(8,128)(2,1)S(1)} %broadcast_in_dim.6), channel_id=1, replica_groups=mesh['tile'=16,'depth'=16] {'depth'}, dimensions={0} | all-to-all | bytes 1048576 | tf_op jit(solution)/shard_map/all_to_all | solution.py:40
  211.3 0.8 copy.33
  (30 shorter events, 1.3 us)
Async XLA Ops:
  5.7 2.2 %copy-start = (bf16[1,1,128,128,128]{4,3,2,1,0:T(8,128)(2,1)S(1)}, bf16[1,1,128,128,128]{4,3,2,1,0:T(8,128)(2,1)}, u32[]{:S(2)}) copy-start(bf16[1,1,128,128,128]{4,3,2,1,0:T(8,128)(2,1)} %param.10) | copy-start | bytes 12582916
  92.8 7.8 %copy-start.4 = (u32[256]{0:T(256)S(1)}, u32[256]{0:T(256)}, u32[]{:S(2)}) copy-start(u32[256]{0:T(256)} %constant.38) | copy-start | bytes 3076
  92.8 9.0 %copy-start.1 = (s32[1,1,16,16]{3,2,1,0:T(8,128)S(1)}, s32[1,1,16,16]{3,2,1,0:T(8,128)}, u32[]{:S(2)}) copy-start(s32[1,1,16,16]{3,2,1,0:T(8,128)} %param.16) | copy-start | bytes 3076
  92.8 38.4 %all-to-all-start = ((bf16[16,4,16384]{2,1,0:T(4,128)(2,1)}), bf16[16,4,16384]{2,1,0:T(4,128)(2,1)}, u32[]{:S(2)}, u32[]{:S(2)}) async-start(bf16[16,4,16384]{2,1,0:T(4,128)(2,1)} %reshape.141), calls=%async_computation | async-start | bytes 4194304 | tf_op jit(solution)/shard_map/all_to_all | solution.py:222
  147.6 13.9 %copy-start.2 = (s32[16]{0:T(128)S(1)}, s32[16]{0:T(128)}, u32[]{:S(2)}) copy-start(s32[16]{0:T(128)} %param.19) | copy-start | bytes 196
  147.6 13.9 %copy-start.3 = (s32[16]{0:T(128)S(1)}, s32[16]{0:T(128)}, u32[]{:S(2)}) copy-start(s32[16]{0:T(128)} %param.18) | copy-start | bytes 196
  149.2 40.2 %all-to-all-start.1 = ((f32[4,16,4096]{2,0,1:T(4,128)}), f32[4,16,4096]{2,0,1:T(4,128)S(1)}, u32[]{:S(2)}, u32[]{:S(2)}) async-start(f32[4,16,4096]{2,0,1:T(4,128)} %copy.32), calls=%async_computation.1 | async-start | bytes 2097152 | tf_op jit(solution)/shard_map/all_to_all | solution.py:252

commit v2 on v1

v2 whole, which is shorter than its diff:
```python
import math
import jax
import jax.numpy as jnp
import numpy as np
from jax import lax
from jax.experimental import pallas as pl
from jax.experimental.pallas import tpu as pltpu
from jax.sharding import PartitionSpec as P

SAMPLES = 128
RAYS = 256
SIDE = 128
STEP = 8
BLOCKS = SAMPLES // STEP
ROWS = RAYS // STEP
LOG2E = math.log2(math.e)
GROUP = 16
DEVICES = 256
VMEM_LIMIT = 48 * 2**20
F32 = jnp.float32
BF16 = jnp.bfloat16


def iota(shape, dim):
    return lax.broadcasted_iota(jnp.int32, shape, dim)


def bits(value, shift, mask):
    return jnp.bitwise_and(jnp.right_shift(value, shift), mask)


def ones_where(condition):
    return jnp.where(condition, 1.0, 0.0).astype(BF16)


def spline(offset):
    size_abs = jnp.abs(offset)
    inner = 2.0 / 3.0 - size_abs * size_abs + 0.5 * size_abs * size_abs * size_abs
    remain = 2.0 - size_abs
    outer = remain * remain * remain / 6.0
    return jnp.where(size_abs < 1.0, inner, jnp.where(size_abs < 2.0, outer, 0.0))


def wrapped(diff):
    return jnp.bitwise_and(diff + 64, 127) - 64


def band(base, mask_ref):
    base = jnp.concatenate([base, pltpu.roll(base, 8, 1)], 0).astype(BF16)
    parts = []
    for k in range(SIDE // 16):
        part = pltpu.roll(base, 16 * k, 1) if k else base
        if k not in (3, 4):
            part = part * mask_ref[pl.ds(16 * k, 16), :]
        parts.append(part)
    return jnp.concatenate(parts, 0)


def render_kernel(
    shear_ref, rate_ref, slope_ref, bias_ref, live_ref, vol_hbm, out_ref,
    vol_ref, wide_ref, even_ref, odd_ref, cum_ref, clear_ref, acc_ref, mask_ref, plane_ref, pick_ref, sems,
):
    w0 = float(np.float32(2.0 / 3.0).astype(BF16))
    w1 = float(np.float32(1.0 / 6.0).astype(BF16))

    def chunk(k):
        at = pl.ds(k * STEP, STEP)
        return pltpu.make_async_copy(vol_hbm.at[at], vol_ref.at[at], sems.at[k])

    for k in range(BLOCKS):
        chunk(k).start()
    r = iota((SIDE, SIDE), 0)
    c = iota((SIDE, SIDE), 1)
    mask_ref[...] = ones_where(jnp.abs(r - c) < 64)
    cum_ref[...] = jnp.zeros_like(cum_ref)
    clear_ref[...] = jnp.ones_like(clear_ref)
    acc_ref[...] = jnp.zeros_like(acc_ref)
    wide_ref[3] = jnp.zeros((SIDE, SIDE), F32)
    chunk(0).wait()
    wide_ref[0] = vol_ref[0].astype(F32)

    def make_field(field_ref, block, j):
        s = block * STEP + j
        centred = s.astype(F32) - (SIDE - 1) / 2.0
        before = wide_ref[jnp.bitwise_and(s + 3, 3)]
        here = wide_ref[jnp.bitwise_and(s, 3)]
        alive = jnp.where(s == SAMPLES - 1, 0.0, 1.0)
        after = vol_ref[jnp.minimum(s + 1, SAMPLES - 1)].astype(F32) * alive
        wide_ref[jnp.bitwise_and(s + 1, 3)] = after
        cells = (w0 * here + w1 * (before + after)).astype(BF16)
        i = iota((8, SIDE), 0)
        a = iota((8, SIDE), 1)
        d_row = wrapped(i - a).astype(F32)
        d_col = wrapped(a - i).astype(F32)
        shift_r = shear_ref[0] * centred
        shift_c = shear_ref[1] * centred
        rows = jnp.concatenate([band(spline(d_row + (shift_r + q)), mask_ref) for q in (-0.25, 0.25)], 0)
        cols = jnp.concatenate([band(spline(d_col + (shift_c + q)), mask_ref) for q in (-0.25, 0.25)], 1)
        half = jnp.dot(rows, cells, preferred_element_type=F32).astype(BF16)
        field_ref[j] = jnp.dot(half, cols, preferred_element_type=F32)

    def integrate(field_ref, r):
        neg_rate = -LOG2E * rate_ref[0]
        slopes = [0.5 * slope_ref[k] for k in range(3)]
        biases = [0.5 * bias_ref[k] for k in range(3)]
        for sub in range(ROWS // 8):
            at = pl.ds(pl.multiple_of(r * ROWS + 8 * sub, 8), 8)
            cum = cum_ref[at, :]
            clear = clear_ref[at, :]
            acc = [acc_ref[k, at, :] for k in range(3)]
            for j in range(STEP):
                f = field_ref[j, at, :]
                cum = cum + jnp.log(1.0 + jnp.exp2(f * LOG2E))
                after = jnp.exp2(neg_rate * cum)
                w = clear - after
                clear = after
                for k in range(3):
                    acc[k] = acc[k] + w * jnp.tanh(f * slopes[k] + biases[k])
            cum_ref[at, :] = cum
            clear_ref[at, :] = clear
            for k in range(3):
                acc_ref[k, at, :] = acc[k]

    def fused(made_ref, used_ref, block):
        @pl.when(block + 1 < BLOCKS)
        def _():
            chunk(jnp.minimum(block + 1, BLOCKS - 1)).wait()

        @pl.loop(0, STEP)
        def _(r):
            make_field(made_ref, block, r)
            integrate(used_ref, r)

    chunk(1).wait()

    @pl.loop(0, STEP)
    def _(r):
        make_field(even_ref, 0, r)

    @pl.loop(0, BLOCKS // 2 - 1)
    def _(t):
        fused(odd_ref, even_ref, 2 * t + 1)
        fused(even_ref, odd_ref, 2 * t + 2)

    fused(odd_ref, even_ref, BLOCKS - 1)

    @pl.loop(0, STEP)
    def _(r):
        integrate(odd_ref, r)

    col = iota((8, RAYS), 1)
    lane_fv = bits(col, 5, 3)
    alpha = 1.0 - clear_ref[...]
    for k in range(4):
        plane_ref[k] = (alpha if k == 3 else 0.5 * (alpha + acc_ref[k])).astype(BF16)
    for fu in range(4):
        limit = jnp.zeros((8, RAYS), jnp.int32)
        for fv in range(4):
            limit = jnp.where(lane_fv == fv, live_ref[4 * fu + fv], limit)
        limit = jnp.concatenate([limit] * 4, 0)
        for par in range(2):
            at = pl.ds(128 * par + 32 * fu, 32)
            keep = ones_where(2 * iota((32, RAYS), 0) + par < limit)
            for k in range(4):
                plane_ref[k, at, :] = plane_ref[k, at, :] * keep
    lane = iota((1, RAYS), 1)
    src = iota((RAYS, RAYS), 0)
    for k in range(4):
        v = 128 * bits(lane, 7, 1) + 64 * bits(lane, 4, 1) + 16 * bits(bits(lane, 5, 3) - k, 0, 3) + bits(lane, 0, 15)
        select = ones_where(src == bits(v, 0, 1) * 128 + bits(v, 1, 127))
        got = jnp.dot(plane_ref[k], select, preferred_element_type=F32).astype(BF16)
        for fvh in range(2):
            pick_ref[k, fvh] = got[:, 128 * fvh : 128 * fvh + 128]
    turn = ones_where(src == bits(lane, 0, 15) * 16 + bits(lane, 4, 1) * 8 + bits(lane, 5, 7))
    block = bits(iota((16, 128), 1), 5, 3)
    for qb in range(4):
        masks = [ones_where(block == (k + qb) % 4) for k in range(4)]
        for g in range(2):
            stack = []
            for fu in range(4):
                for fvh in range(2):
                    for par in range(2):
                        at = pl.ds(128 * par + 32 * fu + 16 * g, 16)
                        picked = [pick_ref[k, fvh, at, :] * masks[k] for k in range(4)]
                        stack.append((picked[0] + picked[1]) + (picked[2] + picked[3]))
            lines = jnp.dot(turn, jnp.concatenate(stack, 0), preferred_element_type=F32).astype(BF16)
            out_ref[pl.ds((qb * 64 + 32 * g) * 8, 256), :] = lines


def render(brick, shear_pair, rate, slope, bias, live):
    smem = pl.BlockSpec(memory_space=pltpu.SMEM)
    return pl.pallas_call(
        render_kernel,
        in_specs=[smem] * 5 + [pl.BlockSpec(memory_space=pl.ANY)],
        out_specs=pl.BlockSpec(memory_space=pltpu.VMEM),
        out_shape=jax.ShapeDtypeStruct((DEVICES * 8, 128), BF16),
        scratch_shapes=[
            pltpu.VMEM((SAMPLES, SIDE, SIDE), BF16),
            pltpu.VMEM((4, SIDE, SIDE), F32),
            pltpu.VMEM((STEP, RAYS, RAYS), F32),
            pltpu.VMEM((STEP, RAYS, RAYS), F32),
            pltpu.VMEM((RAYS, RAYS), F32),
            pltpu.VMEM((RAYS, RAYS), F32),
            pltpu.VMEM((3, RAYS, RAYS), F32),
            pltpu.VMEM((SIDE, SIDE), BF16),
            pltpu.VMEM((4, RAYS, RAYS), BF16),
            pltpu.VMEM((4, 2, RAYS, 128), BF16),
            pltpu.SemaphoreType.DMA((BLOCKS,)),
        ],
        compiler_params=pltpu.CompilerParams(vmem_limit_bytes=VMEM_LIMIT),
        cost_estimate=pl.CostEstimate(flops=4 * 10**9, transcendentals=50 * 10**6, bytes_accessed=5 * 10**6),
        name="render",
    )(shear_pair, rate, slope, bias, live, brick)


def route_kernel(me_ref, target_ref, owner_ref, perm_ref, out_ref):
    frag = iota((16, 16), 0)
    tile = iota((16, 16), 1)
    target = jnp.broadcast_to(target_ref[...], (16, 16))
    onehot = jnp.where(target == tile, 1.0, 0.0)
    earlier = jnp.where(tile < frag, 1.0, 0.0)
    ahead = jnp.dot(earlier, onehot, preferred_element_type=F32)
    rank = jnp.sum(ahead * onehot, 1, keepdims=True)
    spots = jnp.dot(onehot, perm_ref[...].astype(F32), preferred_element_type=F32)
    position = jnp.sum(jnp.where(tile.astype(F32) == rank, spots, 0.0), 1, keepdims=True).astype(jnp.int32)
    owners = jnp.zeros((16, 16), jnp.int32)
    for t in range(16):
        owners = jnp.where(tile == t, owner_ref[t], owners)
    owner = jnp.sum(jnp.where(target == tile, owners, 0).astype(F32), 1, keepdims=True).astype(jnp.int32)
    key = bits(position, 0, 1) * 128 + owner * 8 + bits(position, 1, 7)
    key = jnp.broadcast_to(key, (16, 128)).astype(F32)
    f = iota((16, 128), 0)
    here = iota((16, 128), 1) == me_ref[0] * 8 + bits(f, 1, 7)
    lines = [
        jnp.sum(jnp.where(here & (bits(f, 0, 1) == f2), key, 0.0), 0, keepdims=True) for f2 in range(2)
    ]
    line = jnp.concatenate(lines, 0).astype(BF16)
    out_ref[...] = jnp.broadcast_to(line[None], (DEVICES, 2, 128))


def route(me, target, owner, perm):
    smem = pl.BlockSpec(memory_space=pltpu.SMEM)
    vmem = pl.BlockSpec(memory_space=pltpu.VMEM)
    return pl.pallas_call(
        route_kernel,
        in_specs=[smem, vmem, smem, vmem],
        out_specs=vmem,
        out_shape=jax.ShapeDtypeStruct((DEVICES, 2, 128), BF16),
        cost_estimate=pl.CostEstimate(flops=10**4, transcendentals=0, bytes_accessed=10**5),
        name="route",
    )(me, target, owner, perm)


def composite_kernel(me_ref, owner_ref, view_ref, key_ref, data_ref, out_ref):
    src = iota((RAYS, 128), 0)
    row_owner = bits(iota((128, 128), 0), 3, 15)
    flip = jnp.zeros((128, 128), jnp.int32)
    for t in range(16):
        flip = jnp.where(row_owner == owner_ref[t], view_ref[t], flip)
    flipped = jnp.concatenate([flip, flip], 0) == 1
    last = bits(3 + jnp.right_shift(me_ref[0], 2), 0, 3)
    lane = iota((1, RAYS), 1)
    channel = jnp.where(bits(lane, 4, 1) == 1, last, bits(lane, 5, 3))
    split = ones_where(iota((128, RAYS), 0) == channel * 32 + bits(lane, 7, 1) * 16 + bits(lane, 0, 15))
    row = iota((RAYS, 128), 0).astype(F32)

    def slab(d, carry):
        color, front = carry
        keys = jnp.sum(key_ref[:, d].astype(F32), 0)
        data = data_ref[:, d].reshape(128, 128)
        value = jnp.dot(data, split, preferred_element_type=F32).astype(BF16)
        value = jnp.concatenate([value[:, :128], value[:, 128:]], 0)
        place = jnp.concatenate([ones_where(row == keys[f2 : f2 + 1]) for f2 in range(2)], 1)
        layer = jnp.dot(place, value, preferred_element_type=F32)
        clear = 1.0 - pltpu.roll(layer, 112, 1)
        color = jnp.where(flipped, layer + clear * color, color + front * layer)
        return color, front * clear

    start = (jnp.zeros((RAYS, 128), F32), jnp.ones((RAYS, 128), F32))
    color, front = lax.fori_loop(0, GROUP, slab, start, unroll=4)
    lane = iota((RAYS, 128), 1)
    final = jnp.where(bits(lane, 5, 3) == last, 1.0 - front, color)
    low = bits(iota((128, 128), 1), 4, 1) == 0
    final = jnp.where(low, final[:128], pltpu.roll(final[128:], 16, 1)).astype(BF16)
    out_ref[...] = jnp.broadcast_to(final.reshape(GROUP, 1, 8, 128), (GROUP, GROUP, 8, 128))


def composite(me, owner, view, keys, data):
    smem = pl.BlockSpec(memory_space=pltpu.SMEM)
    vmem = pl.BlockSpec(memory_space=pltpu.VMEM)
    return pl.pallas_call(
        composite_kernel,
        in_specs=[smem, smem, smem, vmem, vmem],
        out_specs=vmem,
        out_shape=jax.ShapeDtypeStruct((GROUP, GROUP, 8, 128), BF16),
        compiler_params=pltpu.CompilerParams(vmem_limit_bytes=VMEM_LIMIT),
        cost_estimate=pl.CostEstimate(flops=10**9, transcendentals=0, bytes_accessed=10**6),
        name="composite",
    )(me, owner, view, keys.reshape(GROUP, GROUP, 2, 128), data.reshape(GROUP, GROUP, 8, 128))


def assemble_kernel(data_ref, out_ref, wide_ref, spot_ref):
    in_row = iota((1, 128), 1)
    turn = ones_where(iota((128, 128), 0) == bits(in_row, 0, 7) * 16 + bits(in_row, 3, 15))
    for qb in range(4):
        for g in range(4):
            lines = data_ref[pl.ds((qb * 64 + 16 * g) * 8, 128), :]
            lines = jnp.dot(turn, lines, preferred_element_type=F32).astype(BF16)
            for pp in range(8):
                at = pl.ds(64 * (pp // 2) + 16 * g, 16)
                wide_ref[at, pl.ds((qb * 2 + pp % 2) * 128, 128)] = lines[16 * pp : 16 * pp + 16]
    src = iota((128, RAYS), 0)
    v = iota((1, RAYS), 1)
    block = bits(src, 0, 31)
    for qb in range(4):
        for pch in range(2):
            hit = (bits(v, 7, 1) == pch) & (bits(v, 4, 3) == qb)
            at = jnp.where(hit, 16 * bits(v, 6, 1) + bits(v, 0, 15), 32)
            spot_ref[pl.ds((qb * 2 + pch) * 128, 128), :] = ones_where(block == at)
    wide_lane = iota((16, 8 * 128), 1)
    lane_ch = bits(bits(wide_lane, 5, 3) - bits(wide_lane, 8, 3), 0, 3)
    for k in range(4):
        mask = jnp.concatenate([ones_where(lane_ch == k)] * 16, 0)
        out_ref[0, k] = jnp.dot(wide_ref[...] * mask, spot_ref[...], preferred_element_type=F32).astype(BF16)


def assemble(data):
    return pl.pallas_call(
        assemble_kernel,
        in_specs=[pl.BlockSpec(memory_space=pltpu.VMEM)],
        out_specs=pl.BlockSpec(memory_space=pltpu.VMEM),
        out_shape=jax.ShapeDtypeStruct((1, 4, RAYS, RAYS), BF16),
        scratch_shapes=[pltpu.VMEM((RAYS, 1024), BF16), pltpu.VMEM((1024, RAYS), BF16)],
        compiler_params=pltpu.CompilerParams(vmem_limit_bytes=VMEM_LIMIT),
        cost_estimate=pl.CostEstimate(flops=10**9, transcendentals=0, bytes_accessed=10**6),
        name="assemble",
    )(data)


def exchange(blocks):
    return lax.all_to_all(blocks, ("tile", "depth"), split_axis=0, concat_axis=0, tiled=True)


def local(
    volume,
    shear,
    absorb,
    color_slope,
    color_bias,
    frag_tile,
    slot_perm,
    frag_rows,
    tile_view,
    tile_owner,
):
    me = lax.axis_index("tile").reshape(1)
    keys = exchange(route(me, frag_tile[0, 0], tile_owner, slot_perm[0, 0]))
    lines = render(volume[0, 0], shear[0, 0], absorb[0], color_slope, color_bias, frag_rows[0, 0])
    parts = exchange(lines.reshape(DEVICES, 8, 128))
    strips = composite(me, tile_owner, tile_view, keys, parts)
    finished = exchange(strips.reshape(DEVICES, 8, 128))
    return assemble(finished.reshape(DEVICES * 8, 128))


def solution(mesh):
    in_specs = (
        P("tile", "depth", None, None, None),
        P("tile", "depth", None),
        P("tile", "depth"),
        P(),
        P(),
        P("tile", "depth", None, None),
        P("tile", "depth", None, None),
        P("tile", "depth", None),
        P(),
        P(),
    )
    out_specs = P("tile", None, None, None)
    return jax.shard_map(local, mesh=mesh, in_specs=in_specs, out_specs=out_specs, check_vma=False)
```

time: 214 us -> 155 us (0.72)
  waiting for transfers between devices: 26.7 us -> 0.01 us
  blocking collectives: 48.8 us -> 61.6 us
  local copies, waits for them, and re-layouts: 17.3 us -> 6.13 us
  matrix products: 9.86 us -> 0 us
  Pallas kernels: 80.5 us -> 70.9 us
  other arithmetic: 6.93 us -> 0 us
  starting transfers between devices: 20 us -> 15.6 us
    all_to_all x1 -> x2, blocking collectives: 20.4 us -> 61.6 us  [exchange(): lax.all_to_all(blocks, ('tile', 'depth'), split_axis=0, concat_axis=0, ti...]
    unnamed x1 -> x0, blocking collectives: 28.3 us -> none
    all_to_all x2 -> x1, waiting for transfers between devices: 26.7 us -> 0.01 us  [exchange(): lax.all_to_all(blocks, ('tile', 'depth'), split_axis=0, concat_axis=0, ti...]
    dot_general x3 -> x0, matrix products: 9.86 us -> none  [the longest x1 8.93 us: local(): jnp.dot(place, incoming.reshape(group_size * CAP, 4 * FRAG * FRAG), prefe...]
    pallas_call x1 -> x4, Pallas kernels: 80.5 us -> 70.9 us  [the longest x1 63.7 us: render(): pl.pallas_call(render_kernel, in_specs=[smem] * 5 + [pl.BlockSpec(memory_...]
    reshape x4 -> x0, local copies, waits for them, and re-layouts: 8.38 us -> none  [the longest x2 5.74 us: local(): incoming.reshape(group_size * CAP, 4 * FRAG * FRAG)]
    all_to_all x2 -> x1, starting transfers between devices: 20 us -> 15.6 us  [exchange(): lax.all_to_all(blocks, ('tile', 'depth'), split_axis=0, concat_axis=0, ti...]
    another operation x2 -> x0, local copies, waits for them, and re-layouts: 3.17 us -> none  [local(): stacked = tile_image.reshape(4, slab_count, strip_rows * TILE_SIDE)]
  transfers between devices with their start and end apart: 2 -> 1, of which waited for: 1 -> 0; matrix products, arithmetic and copies ran while one was open for 1% -> 0% of each run, Pallas kernels for 0% -> 41%
where the time goes in v2:
time: 155 us
  Pallas kernels  70.9 us (46%)
  blocking collectives  61.6 us (40%)
  starting transfers between devices  15.6 us (10%)
  local copies, waits for them, and re-layouts  6.13 us (4%)
    pallas_call x1, Pallas kernels, render(): pl.pallas_call(render_kernel, in_specs=[smem] * 5 + [pl.BlockSpec(memory_...  63.7 us
    all_to_all x2, blocking collectives, exchange(): lax.all_to_all(blocks, ('tile', 'depth'), split_axis=0, concat_axis=0, ti...  61.6 us
    all_to_all x1, starting transfers between devices, exchange(): lax.all_to_all(blocks, ('tile', 'depth'), split_axis=0, concat_axis=0, ti...  15.6 us
    unnamed x14, local copies, waits for them, and re-layouts  4.81 us
    pallas_call x1, Pallas kernels, composite(): pl.pallas_call(composite_kernel, in_specs=[smem, smem, smem, vmem, vmem],...  3.59 us
  transfers between devices with their start and end apart: 1, of which 0 were waited for; matrix products, arithmetic and copies ran while one was open for 0% of the time, Pallas kernels for 41%

profile of v2, /device:TPU:1, one launch (start us, length us, event | category | flops | bytes accessed | tf_op | source)
XLA Modules:
  0.0 154.9 jit_solution(2677539211139124737)
XLA Ops:
  0.0 1.3 copy.11.target_ref
  1.3 1.9 %route.1 = bf16[256,2,128]{2,1,0:T(2,128)(2,1)} custom-call(s32[1]{0:T(128)} %bitcast.me_ref, s32[16,1]{1,0:T(8,128)} %copy.11.target_ref, s32[16]{0:T(128)} %owner_ref.3, s32[16,16]{1,0:T(8,128)} %bitcast.21), custom_call_target="tpu_custom_call" | custom-call | flops 10000 | bytes 100000 | tf_op jit(solution)/shard_map/route/pallas_call | solution.py:244
  3.2 15.6 %all-to-all-start = ((bf16[256,2,128]{2,1,0:T(2,128)(2,1)}), bf16[256,2,128]{2,1,0:T(2,128)(2,1)S(1)}, u32[]{:S(2)}, u32[]{:S(2)}) async-start(bf16[256,2,128]{2,1,0:T(2,128)(2,1)} %route.1), calls=%async_computation | async-start | bytes 262144 | tf_op jit(solution)/shard_map/all_to_all | solution.py:341
  19.5 0.0 copy-start.1
  19.5 2.2 %copy-done.1 = bf16[1,1,128,128,128]{4,3,2,1,0:T(8,128)(2,1)S(1)} copy-done((bf16[1,1,128,128,128]{4,3,2,1,0:T(8,128)(2,1)S(1)}, bf16[1,1,128,128,128]{4,3,2,1,0:T(8,128)(2,1)}, u32[]{:S(2)}) %copy-start.1) | copy-done | bytes 4194328
  21.7 0.0 copy-start.2
  21.7 0.7 copy-done.2
  22.4 0.0 copy-start.3
  22.4 0.7 copy-done.3
  23.0 0.0 copy-start.4
  23.0 0.7 copy-done.4
  23.7 0.0 copy-start.5
  23.7 0.7 copy-done.5
  24.3 0.0 copy-start
  24.3 0.0 copy-start.6
  24.3 63.7 %render.1 = bf16[2048,128]{1,0:T(8,128)(2,1)S(1)} custom-call(f32[2]{0:T(128)S(1)} %bitcast.19, f32[1]{0:T(128)} %bitcast.12.rate_ref, f32[3]{0:T(128)S(1)} %copy-done.3, f32[3]{0:T(128)S(1)} %copy-done.4, s32[16]{0:T(128)S(1)} %bitcast.20, bf16[128,128,128]{2,1,0:T(8,128)(2,1)S(1)} %bitcast.18), custom_call_target="tpu_custom_call" | custom-call | flops 4000000000 | bytes 5000000 | tf_op jit(solution)/shard_map/render/pallas_call | solution.py:192
  88.1 0.0 all-to-all-done
  88.1 34.9 %all_to_all.15 = bf16[256,8,128]{2,1,0:T(8,128)(2,1)S(1)} all-to-all(bf16[256,8,128]{2,1,0:T(8,128)(2,1)S(1)} %bitcast.13), channel_id=1, replica_groups=mesh['tile'=16,'depth'=16] {'tile','depth'}, dimensions={0} | all-to-all | bytes 1048576 | tf_op jit(solution)/shard_map/all_to_all | solution.py:341
  123.0 0.0 copy-done
  123.0 0.0 copy-done.6
  123.0 3.6 %composite.1 = bf16[16,16,8,128]{3,2,1,0:T(8,128)(2,1)S(1)} custom-call(s32[1]{0:T(128)} %bitcast.me_ref, s32[16]{0:T(128)S(1)} %copy-done, s32[16]{0:T(128)S(1)} %copy-done.6, bf16[16,16,2,128]{3,2,1,0:T(2,128)(2,1)S(1)} %bitcast.17, bf16[16,16,8,128]{3,2,1,0:T(8,128)(2,1)S(1)} %bitcast.14), custom_call_target="tpu_custom_call" | custom-call | flops 1000000000 | bytes 1000000 | tf_op jit(solution)/shard_map/composite/pallas_call | solution.py:291
  126.6 26.6 %all_to_all.16 = bf16[256,8,128]{2,1,0:T(8,128)(2,1)S(1)} all-to-all(bf16[256,8,128]{2,1,0:T(8,128)(2,1)S(1)} %bitcast.15), channel_id=1, replica_groups=mesh['tile'=16,'depth'=16] {'tile','depth'}, dimensions={0} | all-to-all | bytes 1048576 | tf_op jit(solution)/shard_map/all_to_all | solution.py:341
  153.2 1.7 %assemble.1 = bf16[1,4,256,256]{3,2,1,0:T(8,128)(2,1)} custom-call(bf16[2048,128]{1,0:T(8,128)(2,1)S(1)} %bitcast.16), custom_call_target="tpu_custom_call" | custom-call | flops 1000000000 | bytes 1000000 | tf_op jit(solution)/shard_map/assemble/pallas_call | solution.py:328
Async XLA Ops:
  3.2 84.9 %all-to-all-start = ((bf16[256,2,128]{2,1,0:T(2,128)(2,1)}), bf16[256,2,128]{2,1,0:T(2,128)(2,1)S(1)}, u32[]{:S(2)}, u32[]{:S(2)}) async-start(bf16[256,2,128]{2,1,0:T(2,128)(2,1)} %route.1), calls=%async_computation | async-start | bytes 262144 | tf_op jit(solution)/shard_map/all_to_all | solution.py:341
  19.5 2.2 %copy-start.1 = (bf16[1,1,128,128,128]{4,3,2,1,0:T(8,128)(2,1)S(1)}, bf16[1,1,128,128,128]{4,3,2,1,0:T(8,128)(2,1)}, u32[]{:S(2)}) copy-start(bf16[1,1,128,128,128]{4,3,2,1,0:T(8,128)(2,1)} %param.10) | copy-start | bytes 12582916
  21.7 0.7 copy-start.2
  22.4 0.7 copy-start.3
  23.0 0.7 copy-start.4
  23.7 0.7 copy-start.5
  24.3 98.7 %copy-start = (s32[16]{0:T(128)S(1)}, s32[16]{0:T(128)}, u32[]{:S(2)}) copy-start(s32[16]{0:T(128)} %owner_ref.3) | copy-start | bytes 196
  24.3 98.7 %copy-start.6 = (s32[16]{0:T(128)S(1)}, s32[16]{0:T(128)}, u32[]{:S(2)}) copy-start(s32[16]{0:T(128)} %view_ref.1) | copy-start | bytes 196

commit v3 on v2

--- a/solution.py
+++ b/solution.py
@@ -16,6 +16,8 @@
 LOG2E = math.log2(math.e)
 GROUP = 16
 DEVICES = 256
+LINES = 10
+TOGETHER = 4
 VMEM_LIMIT = 48 * 2**20
 F32 = jnp.float32
 BF16 = jnp.bfloat16
@@ -56,10 +58,41 @@
     return jnp.concatenate(parts, 0)
 
 
+def key_lines(me, target_ref, owner_ref, perm):
+    frag = iota((16, 16), 0)
+    tile = iota((16, 16), 1)
+    target = jnp.zeros((16, 16), jnp.int32)
+    owners = jnp.zeros((16, 16), jnp.int32)
+    for t in range(16):
+        target = jnp.where(frag == t, target_ref[t], target)
+        owners = jnp.where(tile == t, owner_ref[t], owners)
+    onehot = jnp.where(target == tile, 1.0, 0.0)
+    earlier = jnp.where(tile < frag, 1.0, 0.0)
+    ahead = jnp.dot(earlier, onehot, preferred_element_type=F32)
+    rank = jnp.sum(ahead * onehot, 1, keepdims=True)
+    spots = jnp.dot(onehot, perm.astype(F32), preferred_element_type=F32)
+    position = jnp.sum(jnp.where(tile.astype(F32) == rank, spots, 0.0), 1, keepdims=True).astype(jnp.int32)
+    owner = jnp.sum(onehot * owners.astype(F32), 1, keepdims=True).astype(jnp.int32)
+    key = bits(position, 0, 1) * 128 + owner * 8 + bits(position, 1, 7)
+    key = jnp.broadcast_to(key, (16, 128)).astype(F32)
+    f = iota((16, 128), 0)
+    here = iota((16, 128), 1) == me * 8 + bits(f, 1, 7)
+    return [jnp.sum(jnp.where(here & (bits(f, 0, 1) == f2), key, 0.0), 0, keepdims=True) for f2 in range(2)]
+
+
 def render_kernel(
-    shear_ref, rate_ref, slope_ref, bias_ref, live_ref, vol_hbm, out_ref,
-    vol_ref, wide_ref, even_ref, odd_ref, cum_ref, clear_ref, acc_ref, mask_ref, plane_ref, pick_ref, sems,
+    me_ref, shear_hbm, rate_hbm, slope_hbm, bias_hbm, live_hbm, target_hbm, owner_hbm, perm_hbm, vol_hbm, out_ref,
+    shear_ref, rate_ref, slope_ref, bias_ref, live_ref, target_ref, owner_ref, perm_ref,
+    vol_ref, wide_ref, even_ref, odd_ref, cum_ref, clear_ref, acc_ref, mask_ref, plane_ref, pick_ref, fill_ref,
+    sems, small_sems,
 ):
+    small = (
+        (shear_hbm, shear_ref), (rate_hbm, rate_ref), (slope_hbm, slope_ref), (bias_hbm, bias_ref),
+        (live_hbm, live_ref), (target_hbm, target_ref), (owner_hbm, owner_ref), (perm_hbm, perm_ref),
+    )
+    small = [pltpu.make_async_copy(src, dst, small_sems.at[k]) for k, (src, dst) in enumerate(small)]
+    for copy in small:
+        copy.start()
     w0 = float(np.float32(2.0 / 3.0).astype(BF16))
     w1 = float(np.float32(1.0 / 6.0).astype(BF16))
 
@@ -76,6 +109,13 @@
     clear_ref[...] = jnp.ones_like(clear_ref)
     acc_ref[...] = jnp.zeros_like(acc_ref)
     wide_ref[3] = jnp.zeros((SIDE, SIDE), F32)
+    for copy in small:
+        copy.wait()
+    key = key_lines(me_ref[0], target_ref, owner_ref, perm_ref[...])
+    from_line = jnp.where(bits(iota((64, 128), 0), 0, 1) == 0, key[0], key[1]).astype(BF16)
+    at = iota((1, 64), 1)
+    spots = ones_where(iota((32 * LINES, 64), 0) == bits(at, 1, 31) * LINES + 8 + bits(at, 0, 1))
+    fill_ref[...] = jnp.dot(spots, from_line, preferred_element_type=F32)
     chunk(0).wait()
     wide_ref[0] = vol_ref[0].astype(F32)
 
@@ -84,7 +124,7 @@
         centred = s.astype(F32) - (SIDE - 1) / 2.0
         before = wide_ref[jnp.bitwise_and(s + 3, 3)]
         here = wide_ref[jnp.bitwise_and(s, 3)]
-        alive = jnp.where(s == SAMPLES - 1, 0.0, 1.0)
+        alive = jnp.where(s >= SAMPLES - 1, 0.0, 1.0)
         after = vol_ref[jnp.minimum(s + 1, SAMPLES - 1)].astype(F32) * alive
         wide_ref[jnp.bitwise_and(s + 1, 3)] = after
         cells = (w0 * here + w1 * (before + after)).astype(BF16)
@@ -100,53 +140,57 @@
         field_ref[j] = jnp.dot(half, cols, preferred_element_type=F32)
 
     def integrate(field_ref, r):
-        neg_rate = -LOG2E * rate_ref[0]
-        slopes = [0.5 * slope_ref[k] for k in range(3)]
-        biases = [0.5 * bias_ref[k] for k in range(3)]
-        for sub in range(ROWS // 8):
-            at = pl.ds(pl.multiple_of(r * ROWS + 8 * sub, 8), 8)
+        neg_rate = -LOG2E * rate_ref[0, 0]
+        slopes = [jnp.full((16, RAYS), 0.5 * slope_ref[k], F32).astype(BF16) for k in range(3)]
+        biases = [jnp.full((16, RAYS), 0.5 * bias_ref[k], F32).astype(BF16) for k in range(3)]
+        for sub in range(ROWS // 16):
+            at = pl.ds(pl.multiple_of(r * ROWS + 16 * sub, 16), 16)
             cum = cum_ref[at, :]
             clear = clear_ref[at, :]
-            acc = [acc_ref[k, at, :] for k in range(3)]
+            terms = [[], [], []]
             for j in range(STEP):
                 f = field_ref[j, at, :]
                 cum = cum + jnp.log(1.0 + jnp.exp2(f * LOG2E))
                 after = jnp.exp2(neg_rate * cum)
-                w = clear - after
+                w = (clear - after).astype(BF16)
                 clear = after
+                f = f.astype(BF16)
                 for k in range(3):
-                    acc[k] = acc[k] + w * jnp.tanh(f * slopes[k] + biases[k])
+                    terms[k].append(w * jnp.tanh(f * slopes[k] + biases[k]))
+                    size = 1
+                    while (j + 1) % (2 * size) == 0:
+                        last = terms[k].pop()
+                        terms[k][-1] = terms[k][-1] + last
+                        size *= 2
             cum_ref[at, :] = cum
             clear_ref[at, :] = clear
             for k in range(3):
-                acc_ref[k, at, :] = acc[k]
+                acc_ref[k, at, :] += terms[k][0].astype(F32)
+
+    def every(body):
+        @pl.loop(0, STEP // TOGETHER)
+        def _(r):
+            for i in range(TOGETHER):
+                body(TOGETHER * r + i)
 
     def fused(made_ref, used_ref, block):
         @pl.when(block + 1 < BLOCKS)
         def _():
             chunk(jnp.minimum(block + 1, BLOCKS - 1)).wait()
 
-        @pl.loop(0, STEP)
-        def _(r):
+        def both(r):
+            integrate(used_ref, r)
             make_field(made_ref, block, r)
-            integrate(used_ref, r)
+
+        every(both)
 
     chunk(1).wait()
-
-    @pl.loop(0, STEP)
-    def _(r):
-        make_field(even_ref, 0, r)
-
-    @pl.loop(0, BLOCKS // 2 - 1)
+    every(lambda r: make_field(even_ref, 0, r))
+
+    @pl.loop(0, BLOCKS // 2)
     def _(t):
         fused(odd_ref, even_ref, 2 * t + 1)
         fused(even_ref, odd_ref, 2 * t + 2)
-
-    fused(odd_ref, even_ref, BLOCKS - 1)
-
-    @pl.loop(0, STEP)
-    def _(r):
-        integrate(odd_ref, r)
 
     col = iota((8, RAYS), 1)
     lane_fv = bits(col, 5, 3)
@@ -171,7 +215,8 @@
         got = jnp.dot(plane_ref[k], select, preferred_element_type=F32).astype(BF16)
         for fvh in range(2):
             pick_ref[k, fvh] = got[:, 128 * fvh : 128 * fvh + 128]
-    turn = ones_where(src == bits(lane, 0, 15) * 16 + bits(lane, 4, 1) * 8 + bits(lane, 5, 7))
+    spot = (bits(lane, 0, 15) * 2 + bits(lane, 4, 1)) * LINES + bits(lane, 5, 7)
+    turn = ones_where(iota((32 * LINES, RAYS), 0) == spot)
     block = bits(iota((16, 128), 1), 5, 3)
     for qb in range(4):
         masks = [ones_where(block == (k + qb) % 4) for k in range(4)]
@@ -183,18 +228,27 @@
                         at = pl.ds(128 * par + 32 * fu + 16 * g, 16)
                         picked = [pick_ref[k, fvh, at, :] * masks[k] for k in range(4)]
                         stack.append((picked[0] + picked[1]) + (picked[2] + picked[3]))
-            lines = jnp.dot(turn, jnp.concatenate(stack, 0), preferred_element_type=F32).astype(BF16)
-            out_ref[pl.ds((qb * 64 + 32 * g) * 8, 256), :] = lines
-
-
-def render(brick, shear_pair, rate, slope, bias, live):
+            lines = jnp.dot(turn, jnp.concatenate(stack, 0), preferred_element_type=F32) + fill_ref[...]
+            out_ref[pl.ds((qb * 64 + 32 * g) * LINES, 32 * LINES), :] = lines.astype(BF16)
+
+
+def render(me, shear_pair, rate, slope, bias, live, target, owner, perm, brick):
     smem = pl.BlockSpec(memory_space=pltpu.SMEM)
+    hbm = pl.BlockSpec(memory_space=pltpu.MemorySpace.HBM)
     return pl.pallas_call(
         render_kernel,
-        in_specs=[smem] * 5 + [pl.BlockSpec(memory_space=pl.ANY)],
+        in_specs=[smem] + [hbm] * 9,
         out_specs=pl.BlockSpec(memory_space=pltpu.VMEM),
-        out_shape=jax.ShapeDtypeStruct((DEVICES * 8, 128), BF16),
+        out_shape=jax.ShapeDtypeStruct((DEVICES * LINES, 128), BF16),
         scratch_shapes=[
+            pltpu.SMEM((2,), F32),
+            pltpu.SMEM((1, 1), F32),
+            pltpu.SMEM((3,), F32),
+            pltpu.SMEM((3,), F32),
+            pltpu.SMEM((16,), jnp.int32),
+            pltpu.SMEM((16,), jnp.int32),
+            pltpu.SMEM((16,), jnp.int32),
+            pltpu.VMEM((16, 16), jnp.int32),
             pltpu.VMEM((SAMPLES, SIDE, SIDE), BF16),
             pltpu.VMEM((4, SIDE, SIDE), F32),
             pltpu.VMEM((STEP, RAYS, RAYS), F32),
@@ -205,53 +259,28 @@
             pltpu.VMEM((SIDE, SIDE), BF16),
             pltpu.VMEM((4, RAYS, RAYS), BF16),
             pltpu.VMEM((4, 2, RAYS, 128), BF16),
+            pltpu.VMEM((32 * LINES, 128), F32),
             pltpu.SemaphoreType.DMA((BLOCKS,)),
+            pltpu.SemaphoreType.DMA((8,)),
         ],
-        compiler_params=pltpu.CompilerParams(vmem_limit_bytes=VMEM_LIMIT),
         cost_estimate=pl.CostEstimate(flops=4 * 10**9, transcendentals=50 * 10**6, bytes_accessed=5 * 10**6),
         name="render",
-    )(shear_pair, rate, slope, bias, live, brick)
-
-
-def route_kernel(me_ref, target_ref, owner_ref, perm_ref, out_ref):
-    frag = iota((16, 16), 0)
-    tile = iota((16, 16), 1)
-    target = jnp.broadcast_to(target_ref[...], (16, 16))
-    onehot = jnp.where(target == tile, 1.0, 0.0)
-    earlier = jnp.where(tile < frag, 1.0, 0.0)
-    ahead = jnp.dot(earlier, onehot, preferred_element_type=F32)
-    rank = jnp.sum(ahead * onehot, 1, keepdims=True)
-    spots = jnp.dot(onehot, perm_ref[...].astype(F32), preferred_element_type=F32)
-    position = jnp.sum(jnp.where(tile.astype(F32) == rank, spots, 0.0), 1, keepdims=True).astype(jnp.int32)
-    owners = jnp.zeros((16, 16), jnp.int32)
-    for t in range(16):
-        owners = jnp.where(tile == t, owner_ref[t], owners)
-    owner = jnp.sum(jnp.where(target == tile, owners, 0).astype(F32), 1, keepdims=True).astype(jnp.int32)
-    key = bits(position, 0, 1) * 128 + owner * 8 + bits(position, 1, 7)
-    key = jnp.broadcast_to(key, (16, 128)).astype(F32)
-    f = iota((16, 128), 0)
-    here = iota((16, 128), 1) == me_ref[0] * 8 + bits(f, 1, 7)
-    lines = [
-        jnp.sum(jnp.where(here & (bits(f, 0, 1) == f2), key, 0.0), 0, keepdims=True) for f2 in range(2)
-    ]
-    line = jnp.concatenate(lines, 0).astype(BF16)
-    out_ref[...] = jnp.broadcast_to(line[None], (DEVICES, 2, 128))
-
-
-def route(me, target, owner, perm):
-    smem = pl.BlockSpec(memory_space=pltpu.SMEM)
-    vmem = pl.BlockSpec(memory_space=pltpu.VMEM)
-    return pl.pallas_call(
-        route_kernel,
-        in_specs=[smem, vmem, smem, vmem],
-        out_specs=vmem,
-        out_shape=jax.ShapeDtypeStruct((DEVICES, 2, 128), BF16),
-        cost_estimate=pl.CostEstimate(flops=10**4, transcendentals=0, bytes_accessed=10**5),
-        name="route",
-    )(me, target, owner, perm)
-
-
-def composite_kernel(me_ref, owner_ref, view_ref, key_ref, data_ref, out_ref):
+    )(me, shear_pair, rate, slope, bias, live, target, owner, perm, brick)
+
+
+def composite_kernel(me_ref, owner_ref, view_ref, data_ref, out_ref, frag_ref, key_ref):
+    at = iota((1, 16 * LINES), 1)
+    from_slab = jnp.right_shift(at * 205, 11)
+    line = at - LINES * from_slab
+    spot = jnp.where(line < 8, from_slab * 8 + line, 128 + (line - 8) * 16 + from_slab)
+    undo = ones_where(iota((16 * LINES, 16 * LINES), 0) == spot)
+    keys = jnp.zeros((32, 128), F32)
+    for i in range(GROUP):
+        lines = data_ref[pl.ds(16 * LINES * i, 16 * LINES), :]
+        lines = jnp.dot(undo, lines, preferred_element_type=F32)
+        frag_ref[i] = lines[:128].reshape(GROUP, 8, 128)
+        keys = keys + lines[128:]
+    key_ref[...] = keys
     src = iota((RAYS, 128), 0)
     row_owner = bits(iota((128, 128), 0), 3, 15)
     flip = jnp.zeros((128, 128), jnp.int32)
@@ -266,11 +295,11 @@
 
     def slab(d, carry):
         color, front = carry
-        keys = jnp.sum(key_ref[:, d].astype(F32), 0)
-        data = data_ref[:, d].reshape(128, 128)
+        keys = [key_ref[pl.ds(16 * f2 + d, 1), :] for f2 in range(2)]
+        data = frag_ref[:, d].reshape(128, 128).astype(BF16)
         value = jnp.dot(data, split, preferred_element_type=F32).astype(BF16)
         value = jnp.concatenate([value[:, :128], value[:, 128:]], 0)
-        place = jnp.concatenate([ones_where(row == keys[f2 : f2 + 1]) for f2 in range(2)], 1)
+        place = jnp.concatenate([ones_where(row == keys[f2]) for f2 in range(2)], 1)
         layer = jnp.dot(place, value, preferred_element_type=F32)
         clear = 1.0 - pltpu.roll(layer, 112, 1)
         color = jnp.where(flipped, layer + clear * color, color + front * layer)
@@ -285,18 +314,19 @@
     out_ref[...] = jnp.broadcast_to(final.reshape(GROUP, 1, 8, 128), (GROUP, GROUP, 8, 128))
 
 
-def composite(me, owner, view, keys, data):
+def composite(me, owner, view, data):
     smem = pl.BlockSpec(memory_space=pltpu.SMEM)
     vmem = pl.BlockSpec(memory_space=pltpu.VMEM)
     return pl.pallas_call(
         composite_kernel,
-        in_specs=[smem, smem, smem, vmem, vmem],
+        in_specs=[smem, smem, smem, vmem],
         out_specs=vmem,
         out_shape=jax.ShapeDtypeStruct((GROUP, GROUP, 8, 128), BF16),
+        scratch_shapes=[pltpu.VMEM((GROUP, GROUP, 8, 128), F32), pltpu.VMEM((32, 128), F32)],
         compiler_params=pltpu.CompilerParams(vmem_limit_bytes=VMEM_LIMIT),
         cost_estimate=pl.CostEstimate(flops=10**9, transcendentals=0, bytes_accessed=10**6),
         name="composite",
-    )(me, owner, view, keys.reshape(GROUP, GROUP, 2, 128), data.reshape(GROUP, GROUP, 8, 128))
+    )(me, owner, view, data)
 
 
 def assemble_kernel(data_ref, out_ref, wide_ref, spot_ref):
@@ -354,10 +384,12 @@
     tile_owner,
 ):
     me = lax.axis_index("tile").reshape(1)
-    keys = exchange(route(me, frag_tile[0, 0], tile_owner, slot_perm[0, 0]))
-    lines = render(volume[0, 0], shear[0, 0], absorb[0], color_slope, color_bias, frag_rows[0, 0])
-    parts = exchange(lines.reshape(DEVICES, 8, 128))
-    strips = composite(me, tile_owner, tile_view, keys, parts)
+    lines = render(
+        me, shear[0, 0], absorb, color_slope, color_bias, frag_rows[0, 0],
+        frag_tile.reshape(16), tile_owner, slot_perm[0, 0], volume[0, 0],
+    )
+    parts = exchange(lines.reshape(DEVICES, LINES // 2, 2, 128))
+    strips = composite(me, tile_owner, tile_view, parts.reshape(DEVICES * LINES, 128))
     finished = exchange(strips.reshape(DEVICES, 8, 128))
     return assemble(finished.reshape(DEVICES * 8, 128))
 

time: 155 us -> 114 us (0.74)
  Pallas kernels: 70.9 us -> 46.7 us
  starting transfers between devices: 15.6 us -> 0 us
  local copies, waits for them, and re-layouts: 6.13 us -> 0.01 us
  blocking collectives: 61.6 us -> 66.1 us
    pallas_call x3 -> x2, Pallas kernels: 69.2 us -> 45 us  [the longest x1 40.9 us: render(): pl.pallas_call(render_kernel, in_specs=[smem] + [hbm] * 9, out_specs=pl.B...]
    all_to_all x1 -> x0, starting transfers between devices: 15.6 us -> none  [exchange(): lax.all_to_all(blocks, ('tile', 'depth'), split_axis=0, concat_axis=0, ti...]
    unnamed x14 -> x4, local copies, waits for them, and re-layouts: 4.81 us -> 0.01 us
    all_to_all x2, blocking collectives: 61.6 us -> 66.1 us  [exchange(): lax.all_to_all(blocks, ('tile', 'depth'), split_axis=0, concat_axis=0, ti...]
  transfers between devices with their start and end apart: 1 -> 0, of which waited for: 0 -> 0; matrix products, arithmetic and copies ran while one was open for 0% -> 0% of each run, Pallas kernels for 41% -> 0%
where the time goes in v3:
time: 114 us; the launch traced here: 113 us
  blocking collectives  66.1 us (58%)
  Pallas kernels  46.7 us (41%)
    all_to_all x2, blocking collectives, exchange(): lax.all_to_all(blocks, ('tile', 'depth'), split_axis=0, concat_axis=0, ti...  66.1 us
    pallas_call x1, Pallas kernels, render(): pl.pallas_call(render_kernel, in_specs=[smem] + [hbm] * 9, out_specs=pl.B...  40.9 us
    pallas_call x1, Pallas kernels, composite(): pl.pallas_call(composite_kernel, in_specs=[smem, smem, smem, vmem], out_s...  4.05 us

profile of v3, /device:TPU:1, one launch (start us, length us, event | category | flops | bytes accessed | tf_op | source)
XLA Modules:
  0.0 113.5 jit_solution(7618790659499357837)
XLA Ops:
  0.7 0.0 copy-start
  0.7 0.0 copy-start.1
  0.7 40.9 %render.1 = bf16[2560,128]{1,0:T(8,128)(2,1)} custom-call(s32[1]{0:T(128)} %bitcast.me_ref, f32[2]{0:T(128)} %bitcast.16, f32[1,1]{1,0:T(1,128)S(6)} %copy.11.rate_hbm, f32[3]{0:T(128)} %slope_hbm.1, f32[3]{0:T(128)} %bias_hbm.1, s32[16]{0:T(128)} %bitcast.17, s32[16]{0:T(128)} %bitcast.18, s32[16]{0:T(128)} %owner_ref.1, s32[16,16]{1,0:T(8,128)} %bitcast.15, ...), custom_call_target="tpu_custom_call" | custom-call | flops 4000000000 | bytes 5000000 | tf_op jit(solution)/shard_map/render/pallas_call | solution.py:238
  41.6 39.8 %all_to_all.10 = bf16[256,5,2,128]{3,2,1,0:T(2,128)(2,1)S(1)} all-to-all(bf16[256,5,2,128]{3,2,1,0:T(2,128)(2,1)} %bitcast.13), channel_id=1, replica_groups=mesh['tile'=16,'depth'=16] {'tile','depth'}, dimensions={0} | all-to-all | bytes 1310720 | tf_op jit(solution)/shard_map/all_to_all | solution.py:371
  81.4 0.0 copy-done
  81.4 0.0 copy-done.1
  81.4 4.0 %composite.1 = bf16[16,16,8,128]{3,2,1,0:T(8,128)(2,1)S(1)} custom-call(s32[1]{0:T(128)} %bitcast.me_ref, s32[16]{0:T(128)S(1)} %copy-done, s32[16]{0:T(128)S(1)} %copy-done.1, bf16[2560,128]{1,0:T(8,128)(2,1)S(1)} %bitcast.10), custom_call_target="tpu_custom_call" | custom-call | flops 1000000000 | bytes 1000000 | tf_op jit(solution)/shard_map/composite/pallas_call | solution.py:320
  85.4 26.4 %all_to_all.11 = bf16[256,8,128]{2,1,0:T(8,128)(2,1)S(1)} all-to-all(bf16[256,8,128]{2,1,0:T(8,128)(2,1)S(1)} %bitcast.11), channel_id=1, replica_groups=mesh['tile'=16,'depth'=16] {'tile','depth'}, dimensions={0} | all-to-all | bytes 1048576 | tf_op jit(solution)/shard_map/all_to_all | solution.py:371
  111.8 1.7 %assemble.1 = bf16[1,4,256,256]{3,2,1,0:T(8,128)(2,1)} custom-call(bf16[2048,128]{1,0:T(8,128)(2,1)S(1)} %bitcast.12), custom_call_target="tpu_custom_call" | custom-call | flops 1000000000 | bytes 1000000 | tf_op jit(solution)/shard_map/assemble/pallas_call | solution.py:358
Async XLA Ops:
  0.7 80.7 %copy-start = (s32[16]{0:T(128)S(1)}, s32[16]{0:T(128)}, u32[]{:S(2)}) copy-start(s32[16]{0:T(128)} %owner_ref.1) | copy-start | bytes 196
  0.7 80.7 %copy-start.1 = (s32[16]{0:T(128)S(1)}, s32[16]{0:T(128)}, u32[]{:S(2)}) copy-start(s32[16]{0:T(128)} %view_ref.1) | copy-start | bytes 196

commit v4 on v3

--- a/solution.py
+++ b/solution.py
@@ -93,8 +93,8 @@
     small = [pltpu.make_async_copy(src, dst, small_sems.at[k]) for k, (src, dst) in enumerate(small)]
     for copy in small:
         copy.start()
-    w0 = float(np.float32(2.0 / 3.0).astype(BF16))
-    w1 = float(np.float32(1.0 / 6.0).astype(BF16))
+    w0 = LOG2E * float(np.float32(2.0 / 3.0).astype(BF16))
+    w1 = LOG2E * float(np.float32(1.0 / 6.0).astype(BF16))
 
     def chunk(k):
         at = pl.ds(k * STEP, STEP)
@@ -109,6 +109,7 @@
     clear_ref[...] = jnp.ones_like(clear_ref)
     acc_ref[...] = jnp.zeros_like(acc_ref)
     wide_ref[3] = jnp.zeros((SIDE, SIDE), F32)
+    vol_ref[SAMPLES] = jnp.zeros((SIDE, SIDE), BF16)
     for copy in small:
         copy.wait()
     key = key_lines(me_ref[0], target_ref, owner_ref, perm_ref[...])
@@ -124,8 +125,7 @@
         centred = s.astype(F32) - (SIDE - 1) / 2.0
         before = wide_ref[jnp.bitwise_and(s + 3, 3)]
         here = wide_ref[jnp.bitwise_and(s, 3)]
-        alive = jnp.where(s >= SAMPLES - 1, 0.0, 1.0)
-        after = vol_ref[jnp.minimum(s + 1, SAMPLES - 1)].astype(F32) * alive
+        after = vol_ref[jnp.minimum(s + 1, SAMPLES)].astype(F32)
         wide_ref[jnp.bitwise_and(s + 1, 3)] = after
         cells = (w0 * here + w1 * (before + after)).astype(BF16)
         i = iota((8, SIDE), 0)
@@ -140,32 +140,29 @@
         field_ref[j] = jnp.dot(half, cols, preferred_element_type=F32)
 
     def integrate(field_ref, r):
-        neg_rate = -LOG2E * rate_ref[0, 0]
-        slopes = [jnp.full((16, RAYS), 0.5 * slope_ref[k], F32).astype(BF16) for k in range(3)]
-        biases = [jnp.full((16, RAYS), 0.5 * bias_ref[k], F32).astype(BF16) for k in range(3)]
-        for sub in range(ROWS // 16):
+        neg_rate = -rate_ref[0, 0]
+        slopes = [jnp.full((16, 128), (0.5 / LOG2E) * slope_ref[k], F32).astype(BF16) for k in range(3)]
+        biases = [jnp.full((16, 128), 0.5 * bias_ref[k], F32).astype(BF16) for k in range(3)]
+        for part in range(2 * (ROWS // 16)):
+            sub, side = part // 2, pl.ds(128 * (part % 2), 128)
             at = pl.ds(pl.multiple_of(r * ROWS + 16 * sub, 16), 16)
-            cum = cum_ref[at, :]
-            clear = clear_ref[at, :]
+            cum = cum_ref[at, side]
+            clear = clear_ref[at, side]
             terms = [[], [], []]
             for j in range(STEP):
-                f = field_ref[j, at, :]
-                cum = cum + jnp.log(1.0 + jnp.exp2(f * LOG2E))
+                f = field_ref[j, at, side]
+                cum = cum + lax.log2(1.0 + jnp.exp2(f))
                 after = jnp.exp2(neg_rate * cum)
                 w = (clear - after).astype(BF16)
                 clear = after
                 f = f.astype(BF16)
                 for k in range(3):
-                    terms[k].append(w * jnp.tanh(f * slopes[k] + biases[k]))
-                    size = 1
-                    while (j + 1) % (2 * size) == 0:
-                        last = terms[k].pop()
-                        terms[k][-1] = terms[k][-1] + last
-                        size *= 2
-            cum_ref[at, :] = cum
-            clear_ref[at, :] = clear
+                    term = w * jnp.tanh(f * slopes[k] + biases[k])
+                    terms[k] = [terms[k][0] + term] if terms[k] else [term]
+            cum_ref[at, side] = cum
+            clear_ref[at, side] = clear
             for k in range(3):
-                acc_ref[k, at, :] += terms[k][0].astype(F32)
+                acc_ref[k, at, side] += terms[k][0].astype(F32)
 
     def every(body):
         @pl.loop(0, STEP // TOGETHER)
@@ -249,7 +246,7 @@
             pltpu.SMEM((16,), jnp.int32),
             pltpu.SMEM((16,), jnp.int32),
             pltpu.VMEM((16, 16), jnp.int32),
-            pltpu.VMEM((SAMPLES, SIDE, SIDE), BF16),
+            pltpu.VMEM((SAMPLES + 1, SIDE, SIDE), BF16),
             pltpu.VMEM((4, SIDE, SIDE), F32),
             pltpu.VMEM((STEP, RAYS, RAYS), F32),
             pltpu.VMEM((STEP, RAYS, RAYS), F32),
@@ -268,7 +265,7 @@
     )(me, shear_pair, rate, slope, bias, live, target, owner, perm, brick)
 
 
-def composite_kernel(me_ref, owner_ref, view_ref, data_ref, out_ref, frag_ref, key_ref):
+def composite_kernel(me_ref, owner_ref, view_ref, data_ref, out_ref, frag_ref, key_ref, layer_ref, flip_ref, color_ref, front_ref):
     at = iota((1, 16 * LINES), 1)
     from_slab = jnp.right_shift(at * 205, 11)
     line = at - LINES * from_slab
@@ -286,27 +283,38 @@
     flip = jnp.zeros((128, 128), jnp.int32)
     for t in range(16):
         flip = jnp.where(row_owner == owner_ref[t], view_ref[t], flip)
-    flipped = jnp.concatenate([flip, flip], 0) == 1
+    flip_ref[...] = jnp.concatenate([flip, flip], 0)
     last = bits(3 + jnp.right_shift(me_ref[0], 2), 0, 3)
     lane = iota((1, RAYS), 1)
     channel = jnp.where(bits(lane, 4, 1) == 1, last, bits(lane, 5, 3))
     split = ones_where(iota((128, RAYS), 0) == channel * 32 + bits(lane, 7, 1) * 16 + bits(lane, 0, 15))
-    row = iota((RAYS, 128), 0).astype(F32)
-
-    def slab(d, carry):
-        color, front = carry
-        keys = [key_ref[pl.ds(16 * f2 + d, 1), :] for f2 in range(2)]
-        data = frag_ref[:, d].reshape(128, 128).astype(BF16)
-        value = jnp.dot(data, split, preferred_element_type=F32).astype(BF16)
-        value = jnp.concatenate([value[:, :128], value[:, 128:]], 0)
-        place = jnp.concatenate([ones_where(row == keys[f2]) for f2 in range(2)], 1)
-        layer = jnp.dot(place, value, preferred_element_type=F32)
-        clear = 1.0 - pltpu.roll(layer, 112, 1)
-        color = jnp.where(flipped, layer + clear * color, color + front * layer)
-        return color, front * clear
-
-    start = (jnp.zeros((RAYS, 128), F32), jnp.ones((RAYS, 128), F32))
-    color, front = lax.fori_loop(0, GROUP, slab, start, unroll=4)
+    row = iota((RAYS, 128), 0).astype(F32).astype(BF16)
+    one, none = jnp.ones((RAYS, 128), BF16), jnp.zeros((RAYS, 128), BF16)
+
+    @pl.loop(0, GROUP // 4)
+    def _(t):
+        for d in [4 * t + i for i in range(4)]:
+            keys = [key_ref[pl.ds(16 * f2 + d, 1), :] for f2 in range(2)]
+            data = frag_ref[:, d].reshape(128, 128).astype(BF16)
+            value = jnp.dot(data, split, preferred_element_type=F32).astype(BF16)
+            value = jnp.concatenate([value[:, :128], value[:, 128:]], 0)
+            place = jnp.concatenate([jnp.where(row == keys[f2].astype(BF16), one, none) for f2 in range(2)], 1)
+            layer_ref[d] = jnp.dot(place, value, preferred_element_type=F32)
+
+    @pl.loop(0, RAYS // 64)
+    def _(t):
+        at = pl.ds(pl.multiple_of(64 * t, 64), 64)
+        flipped = flip_ref[at, :] == 1
+        color, front = jnp.zeros((64, 128), F32), jnp.ones((64, 128), F32)
+        for d in range(GROUP):
+            layer = layer_ref[d, at, :]
+            clear = 1.0 - pltpu.roll(layer, 112, 1)
+            color = jnp.where(flipped, layer + clear * color, color + front * layer)
+            front = front * clear
+        color_ref[at, :] = color
+        front_ref[at, :] = front
+
+    color, front = color_ref[...], front_ref[...]
     lane = iota((RAYS, 128), 1)
     final = jnp.where(bits(lane, 5, 3) == last, 1.0 - front, color)
     low = bits(iota((128, 128), 1), 4, 1) == 0
@@ -322,7 +330,14 @@
         in_specs=[smem, smem, smem, vmem],
         out_specs=vmem,
         out_shape=jax.ShapeDtypeStruct((GROUP, GROUP, 8, 128), BF16),
-        scratch_shapes=[pltpu.VMEM((GROUP, GROUP, 8, 128), F32), pltpu.VMEM((32, 128), F32)],
+        scratch_shapes=[
+            pltpu.VMEM((GROUP, GROUP, 8, 128), F32),
+            pltpu.VMEM((32, 128), F32),
+            pltpu.VMEM((GROUP, RAYS, 128), F32),
+            pltpu.VMEM((RAYS, 128), jnp.int32),
+            pltpu.VMEM((RAYS, 128), F32),
+            pltpu.VMEM((RAYS, 128), F32),
+        ],
         compiler_params=pltpu.CompilerParams(vmem_limit_bytes=VMEM_LIMIT),
         cost_estimate=pl.CostEstimate(flops=10**9, transcendentals=0, bytes_accessed=10**6),
         name="composite",

time: 114 us -> 112 us (0.982)
  Pallas kernels: 46.7 us -> 44.6 us
    pallas_call x1, Pallas kernels: 40.9 us -> 38.5 us  [render(): pl.pallas_call(render_kernel, in_specs=[smem] + [hbm] * 9, out_specs=pl.B...]
where the time goes in v4:
time: 112 us; the launch traced here: 111 us
  blocking collectives  66.1 us (59%)
  Pallas kernels  44.6 us (40%)
    all_to_all x2, blocking collectives, exchange(): lax.all_to_all(blocks, ('tile', 'depth'), split_axis=0, concat_axis=0, ti...  66.1 us
    pallas_call x1, Pallas kernels, render(): pl.pallas_call(render_kernel, in_specs=[smem] + [hbm] * 9, out_specs=pl.B...  38.5 us
    pallas_call x1, Pallas kernels, composite(): pl.pallas_call(composite_kernel, in_specs=[smem, smem, smem, vmem], out_s...  4.45 us

profile of v4, /device:TPU:1, one launch (start us, length us, event | category | flops | bytes accessed | tf_op | source)
XLA Modules:
  0.0 111.4 jit_solution(1736262237622078068)
XLA Ops:
  0.7 0.0 copy-start
  0.7 0.0 copy-start.1
  0.7 38.5 %render.1 = bf16[2560,128]{1,0:T(8,128)(2,1)} custom-call(s32[1]{0:T(128)} %bitcast.me_ref, f32[2]{0:T(128)} %bitcast.16, f32[1,1]{1,0:T(1,128)S(6)} %copy.11.rate_hbm, f32[3]{0:T(128)} %slope_hbm.1, f32[3]{0:T(128)} %bias_hbm.1, s32[16]{0:T(128)} %bitcast.17, s32[16]{0:T(128)} %bitcast.18, s32[16]{0:T(128)} %owner_ref.1, s32[16,16]{1,0:T(8,128)} %bitcast.15, ...), custom_call_target="tpu_custom_call" | custom-call | flops 4000000000 | bytes 5000000 | tf_op jit(solution)/shard_map/render/pallas_call | solution.py:235
  39.2 39.8 %all_to_all.10 = bf16[256,5,2,128]{3,2,1,0:T(2,128)(2,1)S(1)} all-to-all(bf16[256,5,2,128]{3,2,1,0:T(2,128)(2,1)} %bitcast.13), channel_id=1, replica_groups=mesh['tile'=16,'depth'=16] {'tile','depth'}, dimensions={0} | all-to-all | bytes 1310720 | tf_op jit(solution)/shard_map/all_to_all | solution.py:386
  78.9 0.0 copy-done
  78.9 0.0 copy-done.1
  78.9 4.4 %composite.1 = bf16[16,16,8,128]{3,2,1,0:T(8,128)(2,1)S(1)} custom-call(s32[1]{0:T(128)} %bitcast.me_ref, s32[16]{0:T(128)S(1)} %copy-done, s32[16]{0:T(128)S(1)} %copy-done.1, bf16[2560,128]{1,0:T(8,128)(2,1)S(1)} %bitcast.10), custom_call_target="tpu_custom_call" | custom-call | flops 1000000000 | bytes 1000000 | tf_op jit(solution)/shard_map/composite/pallas_call | solution.py:328
  83.4 26.4 %all_to_all.11 = bf16[256,8,128]{2,1,0:T(8,128)(2,1)S(1)} all-to-all(bf16[256,8,128]{2,1,0:T(8,128)(2,1)S(1)} %bitcast.11), channel_id=1, replica_groups=mesh['tile'=16,'depth'=16] {'tile','depth'}, dimensions={0} | all-to-all | bytes 1048576 | tf_op jit(solution)/shard_map/all_to_all | solution.py:386
  109.7 1.7 %assemble.1 = bf16[1,4,256,256]{3,2,1,0:T(8,128)(2,1)} custom-call(bf16[2048,128]{1,0:T(8,128)(2,1)S(1)} %bitcast.12), custom_call_target="tpu_custom_call" | custom-call | flops 1000000000 | bytes 1000000 | tf_op jit(solution)/shard_map/assemble/pallas_call | solution.py:373
Async XLA Ops:
  0.7 78.3 %copy-start = (s32[16]{0:T(128)S(1)}, s32[16]{0:T(128)}, u32[]{:S(2)}) copy-start(s32[16]{0:T(128)} %owner_ref.1) | copy-start | bytes 196
  0.7 78.2 %copy-start.1 = (s32[16]{0:T(128)S(1)}, s32[16]{0:T(128)}, u32[]{:S(2)}) copy-start(s32[16]{0:T(128)} %view_ref.1) | copy-start | bytes 196

commit v5 on v3

--- a/solution.py
+++ b/solution.py
@@ -5,7 +5,7 @@
 from jax import lax
 from jax.experimental import pallas as pl
 from jax.experimental.pallas import tpu as pltpu
-from jax.sharding import PartitionSpec as P
+from jax.sharding import Mesh, PartitionSpec as P
 
 SAMPLES = 128
 RAYS = 256
@@ -16,6 +16,7 @@
 LOG2E = math.log2(math.e)
 GROUP = 16
 DEVICES = 256
+CHIPS = 8
 LINES = 10
 TOGETHER = 4
 VMEM_LIMIT = 48 * 2**20
@@ -93,8 +94,8 @@
     small = [pltpu.make_async_copy(src, dst, small_sems.at[k]) for k, (src, dst) in enumerate(small)]
     for copy in small:
         copy.start()
-    w0 = float(np.float32(2.0 / 3.0).astype(BF16))
-    w1 = float(np.float32(1.0 / 6.0).astype(BF16))
+    w0 = LOG2E * float(np.float32(2.0 / 3.0).astype(BF16))
+    w1 = LOG2E * float(np.float32(1.0 / 6.0).astype(BF16))
 
     def chunk(k):
         at = pl.ds(k * STEP, STEP)
@@ -109,6 +110,7 @@
     clear_ref[...] = jnp.ones_like(clear_ref)
     acc_ref[...] = jnp.zeros_like(acc_ref)
     wide_ref[3] = jnp.zeros((SIDE, SIDE), F32)
+    vol_ref[SAMPLES] = jnp.zeros((SIDE, SIDE), BF16)
     for copy in small:
         copy.wait()
     key = key_lines(me_ref[0], target_ref, owner_ref, perm_ref[...])
@@ -124,8 +126,7 @@
         centred = s.astype(F32) - (SIDE - 1) / 2.0
         before = wide_ref[jnp.bitwise_and(s + 3, 3)]
         here = wide_ref[jnp.bitwise_and(s, 3)]
-        alive = jnp.where(s >= SAMPLES - 1, 0.0, 1.0)
-        after = vol_ref[jnp.minimum(s + 1, SAMPLES - 1)].astype(F32) * alive
+        after = vol_ref[jnp.minimum(s + 1, SAMPLES)].astype(F32)
         wide_ref[jnp.bitwise_and(s + 1, 3)] = after
         cells = (w0 * here + w1 * (before + after)).astype(BF16)
         i = iota((8, SIDE), 0)
@@ -140,17 +141,18 @@
         field_ref[j] = jnp.dot(half, cols, preferred_element_type=F32)
 
     def integrate(field_ref, r):
-        neg_rate = -LOG2E * rate_ref[0, 0]
-        slopes = [jnp.full((16, RAYS), 0.5 * slope_ref[k], F32).astype(BF16) for k in range(3)]
-        biases = [jnp.full((16, RAYS), 0.5 * bias_ref[k], F32).astype(BF16) for k in range(3)]
-        for sub in range(ROWS // 16):
+        neg_rate = -rate_ref[0, 0]
+        slopes = [jnp.full((16, 128), (0.5 / LOG2E) * slope_ref[k], F32).astype(BF16) for k in range(3)]
+        biases = [jnp.full((16, 128), 0.5 * bias_ref[k], F32).astype(BF16) for k in range(3)]
+        for part in range(2 * (ROWS // 16)):
+            sub, side = part // 2, pl.ds(128 * (part % 2), 128)
             at = pl.ds(pl.multiple_of(r * ROWS + 16 * sub, 16), 16)
-            cum = cum_ref[at, :]
-            clear = clear_ref[at, :]
+            cum = cum_ref[at, side]
+            clear = clear_ref[at, side]
             terms = [[], [], []]
             for j in range(STEP):
-                f = field_ref[j, at, :]
-                cum = cum + jnp.log(1.0 + jnp.exp2(f * LOG2E))
+                f = field_ref[j, at, side]
+                cum = cum + lax.log2(1.0 + jnp.exp2(f))
                 after = jnp.exp2(neg_rate * cum)
                 w = (clear - after).astype(BF16)
                 clear = after
@@ -162,10 +164,10 @@
                         last = terms[k].pop()
                         terms[k][-1] = terms[k][-1] + last
                         size *= 2
-            cum_ref[at, :] = cum
-            clear_ref[at, :] = clear
+            cum_ref[at, side] = cum
+            clear_ref[at, side] = clear
             for k in range(3):
-                acc_ref[k, at, :] += terms[k][0].astype(F32)
+                acc_ref[k, at, side] += terms[k][0].astype(F32)
 
     def every(body):
         @pl.loop(0, STEP // TOGETHER)
@@ -249,7 +251,7 @@
             pltpu.SMEM((16,), jnp.int32),
             pltpu.SMEM((16,), jnp.int32),
             pltpu.VMEM((16, 16), jnp.int32),
-            pltpu.VMEM((SAMPLES, SIDE, SIDE), BF16),
+            pltpu.VMEM((SAMPLES + 1, SIDE, SIDE), BF16),
             pltpu.VMEM((4, SIDE, SIDE), F32),
             pltpu.VMEM((STEP, RAYS, RAYS), F32),
             pltpu.VMEM((STEP, RAYS, RAYS), F32),
@@ -311,7 +313,7 @@
     final = jnp.where(bits(lane, 5, 3) == last, 1.0 - front, color)
     low = bits(iota((128, 128), 1), 4, 1) == 0
     final = jnp.where(low, final[:128], pltpu.roll(final[128:], 16, 1)).astype(BF16)
-    out_ref[...] = jnp.broadcast_to(final.reshape(GROUP, 1, 8, 128), (GROUP, GROUP, 8, 128))
+    out_ref[...] = jnp.broadcast_to(final.reshape(GROUP, 1, 8, 128), (GROUP, CHIPS, 8, 128))
 
 
 def composite(me, owner, view, data):
@@ -321,7 +323,7 @@
         composite_kernel,
         in_specs=[smem, smem, smem, vmem],
         out_specs=vmem,
-        out_shape=jax.ShapeDtypeStruct((GROUP, GROUP, 8, 128), BF16),
+        out_shape=jax.ShapeDtypeStruct((GROUP, CHIPS, 8, 128), BF16),
         scratch_shapes=[pltpu.VMEM((GROUP, GROUP, 8, 128), F32), pltpu.VMEM((32, 128), F32)],
         compiler_params=pltpu.CompilerParams(vmem_limit_bytes=VMEM_LIMIT),
         cost_estimate=pl.CostEstimate(flops=10**9, transcendentals=0, bytes_accessed=10**6),
@@ -329,12 +331,14 @@
     )(me, owner, view, data)
 
 
-def assemble_kernel(data_ref, out_ref, wide_ref, spot_ref):
-    in_row = iota((1, 128), 1)
-    turn = ones_where(iota((128, 128), 0) == bits(in_row, 0, 7) * 16 + bits(in_row, 3, 15))
+def assemble_kernel(core_ref, mine_ref, other_ref, out_ref, wide_ref, spot_ref):
+    at = iota((1, 128), 1)
+    row = 2 * bits(at, 3, 7) + jnp.bitwise_xor(bits(at, 6, 1), core_ref[0])
+    turn = ones_where(iota((128, 128), 0) == bits(at, 0, 7) * 16 + row)
     for qb in range(4):
         for g in range(4):
-            lines = data_ref[pl.ds((qb * 64 + 16 * g) * 8, 128), :]
+            at = pl.ds((qb * 4 + g) * 64, 64)
+            lines = jnp.concatenate([mine_ref[at, :], other_ref[at, :]], 0)
             lines = jnp.dot(turn, lines, preferred_element_type=F32).astype(BF16)
             for pp in range(8):
                 at = pl.ds(64 * (pp // 2) + 16 * g, 16)
@@ -354,21 +358,22 @@
         out_ref[0, k] = jnp.dot(wide_ref[...] * mask, spot_ref[...], preferred_element_type=F32).astype(BF16)
 
 
-def assemble(data):
+def assemble(core, mine, other):
+    vmem = pl.BlockSpec(memory_space=pltpu.VMEM)
     return pl.pallas_call(
         assemble_kernel,
-        in_specs=[pl.BlockSpec(memory_space=pltpu.VMEM)],
-        out_specs=pl.BlockSpec(memory_space=pltpu.VMEM),
+        in_specs=[pl.BlockSpec(memory_space=pltpu.SMEM), vmem, vmem],
+        out_specs=vmem,
         out_shape=jax.ShapeDtypeStruct((1, 4, RAYS, RAYS), BF16),
         scratch_shapes=[pltpu.VMEM((RAYS, 1024), BF16), pltpu.VMEM((1024, RAYS), BF16)],
         compiler_params=pltpu.CompilerParams(vmem_limit_bytes=VMEM_LIMIT),
         cost_estimate=pl.CostEstimate(flops=10**9, transcendentals=0, bytes_accessed=10**6),
         name="assemble",
-    )(data)
-
-
-def exchange(blocks):
-    return lax.all_to_all(blocks, ("tile", "depth"), split_axis=0, concat_axis=0, tiled=True)
+    )(core, mine, other)
+
+
+def exchange(blocks, axes):
+    return lax.all_to_all(blocks, axes, split_axis=0, concat_axis=0, tiled=True)
 
 
 def local(
@@ -388,24 +393,26 @@
         me, shear[0, 0], absorb, color_slope, color_bias, frag_rows[0, 0],
         frag_tile.reshape(16), tile_owner, slot_perm[0, 0], volume[0, 0],
     )
-    parts = exchange(lines.reshape(DEVICES, LINES // 2, 2, 128))
+    parts = exchange(lines.reshape(DEVICES, LINES // 2, 2, 128), ("tile", "chip", "core"))
     strips = composite(me, tile_owner, tile_view, parts.reshape(DEVICES * LINES, 128))
-    finished = exchange(strips.reshape(DEVICES, 8, 128))
-    return assemble(finished.reshape(DEVICES * 8, 128))
+    mine = exchange(strips.reshape(GROUP * CHIPS, 8, 128), ("tile", "chip")).reshape(GROUP * CHIPS * 8, 128)
+    other = lax.ppermute(mine, "core", ((0, 1), (1, 0)))
+    return assemble(lax.axis_index("core").reshape(1), mine, other)
 
 
 def solution(mesh):
     in_specs = (
-        P("tile", "depth", None, None, None),
-        P("tile", "depth", None),
-        P("tile", "depth"),
+        P("tile", ("chip", "core"), None, None, None),
+        P("tile", ("chip", "core"), None),
+        P("tile", ("chip", "core")),
         P(),
         P(),
-        P("tile", "depth", None, None),
-        P("tile", "depth", None, None),
-        P("tile", "depth", None),
+        P("tile", ("chip", "core"), None, None),
+        P("tile", ("chip", "core"), None, None),
+        P("tile", ("chip", "core"), None),
         P(),
         P(),
     )
     out_specs = P("tile", None, None, None)
+    mesh = Mesh(mesh.devices.reshape(GROUP, CHIPS, 2), ("tile", "chip", "core"))
     return jax.shard_map(local, mesh=mesh, in_specs=in_specs, out_specs=out_specs, check_vma=False)

time: 114 us -> 108 us (0.947)
  blocking collectives: 66.1 us -> 59.3 us
  Pallas kernels: 46.7 us -> 44.2 us
  starting transfers between devices: 0 us -> 1.95 us
  waiting for transfers between devices: 0 us -> 1.16 us
    all_to_all x2, blocking collectives: 66.1 us -> 59.3 us  [exchange(): return lax.all_to_all(blocks, axes, split_axis=0, concat_axis=0, tiled=True)]
    pallas_call x1, Pallas kernels: 40.9 us -> 38.5 us  [render(): pl.pallas_call(render_kernel, in_specs=[smem] + [hbm] * 9, out_specs=pl.B...]
    ppermute x0 -> x1, starting transfers between devices: none -> 1.95 us  [local(): other = lax.ppermute(mine, 'core', ((0, 1), (1, 0)))]
    ppermute x0 -> x1, waiting for transfers between devices: none -> 1.16 us  [local(): other = lax.ppermute(mine, 'core', ((0, 1), (1, 0)))]
  transfers between devices with their start and end apart: 0 -> 1, of which waited for: 0 -> 1; matrix products, arithmetic and copies ran while one was open for 0% -> 0% of each run, Pallas kernels for 0% -> 0%
where the time goes in v5:
time: 108 us; the launch traced here: 107 us
  blocking collectives  59.3 us (55%)
  Pallas kernels  44.2 us (41%)
  starting transfers between devices  1.95 us (2%)
  waiting for transfers between devices  1.16 us (1%)
    all_to_all x2, blocking collectives, exchange(): return lax.all_to_all(blocks, axes, split_axis=0, concat_axis=0, tiled=True)  59.3 us
    pallas_call x1, Pallas kernels, render(): pl.pallas_call(render_kernel, in_specs=[smem] + [hbm] * 9, out_specs=pl.B...  38.5 us
    pallas_call x1, Pallas kernels, composite(): pl.pallas_call(composite_kernel, in_specs=[smem, smem, smem, vmem], out_s...  4.03 us
  transfers between devices with their start and end apart: 1, of which 1 were waited for; matrix products, arithmetic and copies ran while one was open for 0% of the time, Pallas kernels for 0%

profile of v5, /device:TPU:1, one launch (start us, length us, event | category | flops | bytes accessed | tf_op | source)
XLA Modules:
  0.0 107.3 jit_solution(15567056043709913548)
XLA Ops:
  0.7 0.0 copy-start
  0.7 0.0 copy-start.1
  0.7 38.5 %render.1 = bf16[2560,128]{1,0:T(8,128)(2,1)} custom-call(s32[1]{0:T(128)} %bitcast.1.me_ref, f32[2]{0:T(128)} %bitcast.18, f32[1,1]{1,0:T(1,128)S(6)} %copy.11.rate_hbm, f32[3]{0:T(128)} %slope_hbm.1, f32[3]{0:T(128)} %bias_hbm.1, s32[16]{0:T(128)} %bitcast.19, s32[16]{0:T(128)} %bitcast.20, s32[16]{0:T(128)} %owner_ref.1, s32[16,16]{1,0:T(8,128)} %bitcast.17, ...), custom_call_target="tpu_custom_call" | custom-call | flops 4000000000 | bytes 5000000 | tf_op jit(solution)/shard_map/render/pallas_call | solution.py:240
  39.2 39.8 %all_to_all.10 = bf16[256,5,2,128]{3,2,1,0:T(2,128)(2,1)S(1)} all-to-all(bf16[256,5,2,128]{3,2,1,0:T(2,128)(2,1)} %bitcast.15), channel_id=1, replica_groups=mesh['tile'=16,'chip'=8,'core'=2] {'tile','chip','core'}, dimensions={0} | all-to-all | bytes 1310720 | tf_op jit(solution)/shard_map/all_to_all | solution.py:376
  78.9 0.0 copy-done
  78.9 0.0 copy-done.1
  78.9 4.0 %composite.1 = bf16[16,8,8,128]{3,2,1,0:T(8,128)(2,1)S(1)} custom-call(s32[1]{0:T(128)} %bitcast.1.me_ref, s32[16]{0:T(128)S(1)} %copy-done, s32[16]{0:T(128)S(1)} %copy-done.1, bf16[2560,128]{1,0:T(8,128)(2,1)S(1)} %bitcast.11), custom_call_target="tpu_custom_call" | custom-call | flops 1000000000 | bytes 1000000 | tf_op jit(solution)/shard_map/composite/pallas_call | solution.py:322
  83.0 19.6 %all_to_all.11 = bf16[128,8,128]{2,1,0:T(8,128)(2,1)S(1)} all-to-all(bf16[128,8,128]{2,1,0:T(8,128)(2,1)S(1)} %bitcast.14), channel_id=1, replica_groups=mesh['tile'=16,'chip'=8,'core'=2] {'tile','chip'}, dimensions={0} | all-to-all | bytes 524288 | tf_op jit(solution)/shard_map/all_to_all | solution.py:376
  102.5 1.9 %collective-permute-start = (bf16[1024,128]{1,0:T(8,128)(2,1)S(1)}, bf16[1024,128]{1,0:T(8,128)(2,1)S(1)}, u32[]{:S(2)}, u32[]{:S(2)}) collective-permute-start(bf16[1024,128]{1,0:T(8,128)(2,1)S(1)} %bitcast.12), channel_id=1, source_target_pairs={{0,1},{1,0},{2,3},{3,2},{4,5},{5,4},{6,7},{7,6},{8,9},{9,8},{10,11... | collective-permute-start | bytes 786440 | tf_op jit(solution)/shard_map/ppermute | solution.py:399
  104.5 1.2 %collective-permute-done.other_ref = bf16[1024,128]{1,0:T(8,128)(2,1)S(1)} collective-permute-done((bf16[1024,128]{1,0:T(8,128)(2,1)S(1)}, bf16[1024,128]{1,0:T(8,128)(2,1)S(1)}, u32[]{:S(2)}, u32[]{:S(2)}) %collective-permute-start) | collective-permute-done | bytes 262176 | tf_op jit(solution)/shard_map/ppermute | solution.py:399
  105.7 1.7 %assemble.1 = bf16[1,4,256,256]{3,2,1,0:T(8,128)(2,1)} custom-call(s32[1]{0:T(128)} %bitcast.core_ref, bf16[1024,128]{1,0:T(8,128)(2,1)S(1)} %bitcast.13, bf16[1024,128]{1,0:T(8,128)(2,1)S(1)} %collective-permute-done.other_ref), custom_call_target="tpu_custom_call" | custom-call | flops 1000000000 | bytes 1000000 | tf_op jit(solution)/shard_map/assemble/pallas_call | solution.py:363
Async XLA Ops:
  0.7 78.3 %copy-start = (s32[16]{0:T(128)S(1)}, s32[16]{0:T(128)}, u32[]{:S(2)}) copy-start(s32[16]{0:T(128)} %owner_ref.1) | copy-start | bytes 196
  0.7 78.3 %copy-start.1 = (s32[16]{0:T(128)S(1)}, s32[16]{0:T(128)}, u32[]{:S(2)}) copy-start(s32[16]{0:T(128)} %view_ref.1) | copy-start | bytes 196
  102.5 3.1 %collective-permute-start = (bf16[1024,128]{1,0:T(8,128)(2,1)S(1)}, bf16[1024,128]{1,0:T(8,128)(2,1)S(1)}, u32[]{:S(2)}, u32[]{:S(2)}) collective-permute-start(bf16[1024,128]{1,0:T(8,128)(2,1)S(1)} %bitcast.12), channel_id=1, source_target_pairs={{0,1},{1,0},{2,3},{3,2},{4,5},{5,4},{6,7},{7,6},{8,9},{9,8},{10,11... | collective-permute-start | bytes 786440 | tf_op jit(solution)/shard_map/ppermute | solution.py:399

commit v6 on v5

--- a/solution.py
+++ b/solution.py
@@ -142,8 +142,6 @@
 
     def integrate(field_ref, r):
         neg_rate = -rate_ref[0, 0]
-        slopes = [jnp.full((16, 128), (0.5 / LOG2E) * slope_ref[k], F32).astype(BF16) for k in range(3)]
-        biases = [jnp.full((16, 128), 0.5 * bias_ref[k], F32).astype(BF16) for k in range(3)]
         for part in range(2 * (ROWS // 16)):
             sub, side = part // 2, pl.ds(128 * (part % 2), 128)
             at = pl.ds(pl.multiple_of(r * ROWS + 16 * sub, 16), 16)
@@ -158,7 +156,7 @@
                 clear = after
                 f = f.astype(BF16)
                 for k in range(3):
-                    terms[k].append(w * jnp.tanh(f * slopes[k] + biases[k]))
+                    terms[k].append(w * jnp.tanh(f * slopes[k][j % 4] + biases[k][j % 4]))
                     size = 1
                     while (j + 1) % (2 * size) == 0:
                         last = terms[k].pop()
@@ -168,6 +166,16 @@
             clear_ref[at, side] = clear
             for k in range(3):
                 acc_ref[k, at, side] += terms[k][0].astype(F32)
+
+    def rounded(value):
+        want, have, parts = jnp.full((16, 128), value, F32), jnp.zeros((16, 128), F32), []
+        for n in range(4):
+            parts.append(((n + 1) * want - have).astype(BF16))
+            have = have + parts[-1].astype(F32)
+        return parts
+
+    slopes = [rounded((0.5 / LOG2E) * slope_ref[k]) for k in range(3)]
+    biases = [rounded(0.5 * bias_ref[k]) for k in range(3)]
 
     def every(body):
         @pl.loop(0, STEP // TOGETHER)
@@ -331,7 +339,7 @@
     )(me, owner, view, data)
 
 
-def assemble_kernel(core_ref, mine_ref, other_ref, out_ref, wide_ref, spot_ref):
+def assemble_kernel(core_ref, mine_ref, other_ref, out_ref, wide_ref):
     at = iota((1, 128), 1)
     row = 2 * bits(at, 3, 7) + jnp.bitwise_xor(bits(at, 6, 1), core_ref[0])
     turn = ones_where(iota((128, 128), 0) == bits(at, 0, 7) * 16 + row)
@@ -339,23 +347,23 @@
         for g in range(4):
             at = pl.ds((qb * 4 + g) * 64, 64)
             lines = jnp.concatenate([mine_ref[at, :], other_ref[at, :]], 0)
-            lines = jnp.dot(turn, lines, preferred_element_type=F32).astype(BF16)
+            lines = jnp.dot(turn, lines, preferred_element_type=F32)
             for pp in range(8):
-                at = pl.ds(64 * (pp // 2) + 16 * g, 16)
-                wide_ref[at, pl.ds((qb * 2 + pp % 2) * 128, 128)] = lines[16 * pp : 16 * pp + 16]
-    src = iota((128, RAYS), 0)
+                wide_ref[qb, pp % 2, pl.ds(64 * (pp // 2) + 16 * g, 16), :] = lines[16 * pp : 16 * pp + 16]
+    block = bits(iota((RAYS, 128), 1), 5, 3)
+    src = iota((RAYS, RAYS), 0)
     v = iota((1, RAYS), 1)
-    block = bits(src, 0, 31)
-    for qb in range(4):
+    for k in range(4):
+        parts = []
         for pch in range(2):
-            hit = (bits(v, 7, 1) == pch) & (bits(v, 4, 3) == qb)
-            at = jnp.where(hit, 16 * bits(v, 6, 1) + bits(v, 0, 15), 32)
-            spot_ref[pl.ds((qb * 2 + pch) * 128, 128), :] = ones_where(block == at)
-    wide_lane = iota((16, 8 * 128), 1)
-    lane_ch = bits(bits(wide_lane, 5, 3) - bits(wide_lane, 8, 3), 0, 3)
-    for k in range(4):
-        mask = jnp.concatenate([ones_where(lane_ch == k)] * 16, 0)
-        out_ref[0, k] = jnp.dot(wide_ref[...] * mask, spot_ref[...], preferred_element_type=F32).astype(BF16)
+            part = wide_ref[0, pch]
+            for qb in range(1, 4):
+                part = jnp.where(block == (k + qb) % 4, wide_ref[qb, pch], part)
+            parts.append(part.astype(BF16))
+        at = 128 * bits(v, 7, 1) + 32 * bits(k + bits(v, 4, 3), 0, 3) + 16 * bits(v, 6, 1) + bits(v, 0, 15)
+        out_ref[0, k] = jnp.dot(
+            jnp.concatenate(parts, 1), ones_where(src == at), preferred_element_type=F32
+        ).astype(BF16)
 
 
 def assemble(core, mine, other):
@@ -365,7 +373,7 @@
         in_specs=[pl.BlockSpec(memory_space=pltpu.SMEM), vmem, vmem],
         out_specs=vmem,
         out_shape=jax.ShapeDtypeStruct((1, 4, RAYS, RAYS), BF16),
-        scratch_shapes=[pltpu.VMEM((RAYS, 1024), BF16), pltpu.VMEM((1024, RAYS), BF16)],
+        scratch_shapes=[pltpu.VMEM((4, 2, RAYS, 128), F32)],
         compiler_params=pltpu.CompilerParams(vmem_limit_bytes=VMEM_LIMIT),
         cost_estimate=pl.CostEstimate(flops=10**9, transcendentals=0, bytes_accessed=10**6),
         name="assemble",

time: 108 us -> 108 us (level)
  no operation moved by 1% of the time
where the time goes in v6:
time: 108 us; the launch traced here: 107 us
  blocking collectives  59.3 us (55%)
  Pallas kernels  44.3 us (41%)
  starting transfers between devices  1.95 us (2%)
  waiting for transfers between devices  1.16 us (1%)
    all_to_all x2, blocking collectives, exchange(): return lax.all_to_all(blocks, axes, split_axis=0, concat_axis=0, tiled=True)  59.3 us
    pallas_call x1, Pallas kernels, render(): pl.pallas_call(render_kernel, in_specs=[smem] + [hbm] * 9, out_specs=pl.B...  38.8 us
    pallas_call x1, Pallas kernels, composite(): pl.pallas_call(composite_kernel, in_specs=[smem, smem, smem, vmem], out_s...  4.03 us
  transfers between devices with their start and end apart: 1, of which 1 were waited for; matrix products, arithmetic and copies ran while one was open for 0% of the time, Pallas kernels for 0%

profile of v6, /device:TPU:1, one launch (start us, length us, event | category | flops | bytes accessed | tf_op | source)
XLA Modules:
  0.0 107.5 jit_solution(13670739461623601305)
XLA Ops:
  0.7 0.0 copy-start
  0.7 0.0 copy-start.1
  0.7 38.8 %render.1 = bf16[2560,128]{1,0:T(8,128)(2,1)} custom-call(s32[1]{0:T(128)} %bitcast.1.me_ref, f32[2]{0:T(128)} %bitcast.18, f32[1,1]{1,0:T(1,128)S(6)} %copy.11.rate_hbm, f32[3]{0:T(128)} %slope_hbm.1, f32[3]{0:T(128)} %bias_hbm.1, s32[16]{0:T(128)} %bitcast.19, s32[16]{0:T(128)} %bitcast.20, s32[16]{0:T(128)} %owner_ref.1, s32[16,16]{1,0:T(8,128)} %bitcast.17, ...), custom_call_target="tpu_custom_call" | custom-call | flops 4000000000 | bytes 5000000 | tf_op jit(solution)/shard_map/render/pallas_call | solution.py:248
  39.5 39.8 %all_to_all.10 = bf16[256,5,2,128]{3,2,1,0:T(2,128)(2,1)S(1)} all-to-all(bf16[256,5,2,128]{3,2,1,0:T(2,128)(2,1)} %bitcast.15), channel_id=1, replica_groups=mesh['tile'=16,'chip'=8,'core'=2] {'tile','chip','core'}, dimensions={0} | all-to-all | bytes 1310720 | tf_op jit(solution)/shard_map/all_to_all | solution.py:384
  79.3 0.0 copy-done
  79.3 0.0 copy-done.1
  79.3 4.0 %composite.1 = bf16[16,8,8,128]{3,2,1,0:T(8,128)(2,1)S(1)} custom-call(s32[1]{0:T(128)} %bitcast.1.me_ref, s32[16]{0:T(128)S(1)} %copy-done, s32[16]{0:T(128)S(1)} %copy-done.1, bf16[2560,128]{1,0:T(8,128)(2,1)S(1)} %bitcast.11), custom_call_target="tpu_custom_call" | custom-call | flops 1000000000 | bytes 1000000 | tf_op jit(solution)/shard_map/composite/pallas_call | solution.py:330
  83.3 19.6 %all_to_all.11 = bf16[128,8,128]{2,1,0:T(8,128)(2,1)S(1)} all-to-all(bf16[128,8,128]{2,1,0:T(8,128)(2,1)S(1)} %bitcast.14), channel_id=1, replica_groups=mesh['tile'=16,'chip'=8,'core'=2] {'tile','chip'}, dimensions={0} | all-to-all | bytes 524288 | tf_op jit(solution)/shard_map/all_to_all | solution.py:384
  102.9 1.9 %collective-permute-start = (bf16[1024,128]{1,0:T(8,128)(2,1)S(1)}, bf16[1024,128]{1,0:T(8,128)(2,1)S(1)}, u32[]{:S(2)}, u32[]{:S(2)}) collective-permute-start(bf16[1024,128]{1,0:T(8,128)(2,1)S(1)} %bitcast.12), channel_id=1, source_target_pairs={{0,1},{1,0},{2,3},{3,2},{4,5},{5,4},{6,7},{7,6},{8,9},{9,8},{10,11... | collective-permute-start | bytes 786440 | tf_op jit(solution)/shard_map/ppermute | solution.py:407
  104.8 1.2 %collective-permute-done.other_ref = bf16[1024,128]{1,0:T(8,128)(2,1)S(1)} collective-permute-done((bf16[1024,128]{1,0:T(8,128)(2,1)S(1)}, bf16[1024,128]{1,0:T(8,128)(2,1)S(1)}, u32[]{:S(2)}, u32[]{:S(2)}) %collective-permute-start) | collective-permute-done | bytes 262176 | tf_op jit(solution)/shard_map/ppermute | solution.py:407
  106.0 1.5 %assemble.1 = bf16[1,4,256,256]{3,2,1,0:T(8,128)(2,1)} custom-call(s32[1]{0:T(128)} %bitcast.core_ref, bf16[1024,128]{1,0:T(8,128)(2,1)S(1)} %bitcast.13, bf16[1024,128]{1,0:T(8,128)(2,1)S(1)} %collective-permute-done.other_ref), custom_call_target="tpu_custom_call" | custom-call | flops 1000000000 | bytes 1000000 | tf_op jit(solution)/shard_map/assemble/pallas_call | solution.py:371
Async XLA Ops:
  0.7 78.6 %copy-start = (s32[16]{0:T(128)S(1)}, s32[16]{0:T(128)}, u32[]{:S(2)}) copy-start(s32[16]{0:T(128)} %owner_ref.1) | copy-start | bytes 196
  0.7 78.6 %copy-start.1 = (s32[16]{0:T(128)S(1)}, s32[16]{0:T(128)}, u32[]{:S(2)}) copy-start(s32[16]{0:T(128)} %view_ref.1) | copy-start | bytes 196
  102.9 3.1 %collective-permute-start = (bf16[1024,128]{1,0:T(8,128)(2,1)S(1)}, bf16[1024,128]{1,0:T(8,128)(2,1)S(1)}, u32[]{:S(2)}, u32[]{:S(2)}) collective-permute-start(bf16[1024,128]{1,0:T(8,128)(2,1)S(1)} %bitcast.12), channel_id=1, source_target_pairs={{0,1},{1,0},{2,3},{3,2},{4,5},{5,4},{6,7},{7,6},{8,9},{9,8},{10,11... | collective-permute-start | bytes 786440 | tf_op jit(solution)/shard_map/ppermute | solution.py:407

commit v7 on v6

--- a/solution.py
+++ b/solution.py
@@ -156,7 +156,7 @@
                 clear = after
                 f = f.astype(BF16)
                 for k in range(3):
-                    terms[k].append(w * jnp.tanh(f * slopes[k][j % 4] + biases[k][j % 4]))
+                    terms[k].append(w * jnp.tanh(f * slopes[k][j % 2] + biases[k][j % 2]))
                     size = 1
                     while (j + 1) % (2 * size) == 0:
                         last = terms[k].pop()
@@ -169,7 +169,7 @@
 
     def rounded(value):
         want, have, parts = jnp.full((16, 128), value, F32), jnp.zeros((16, 128), F32), []
-        for n in range(4):
+        for n in range(2):
             parts.append(((n + 1) * want - have).astype(BF16))
             have = have + parts[-1].astype(F32)
         return parts
@@ -200,7 +200,12 @@
     @pl.loop(0, BLOCKS // 2)
     def _(t):
         fused(odd_ref, even_ref, 2 * t + 1)
-        fused(even_ref, odd_ref, 2 * t + 2)
+
+        @pl.when(t < BLOCKS // 2 - 1)
+        def _():
+            fused(even_ref, odd_ref, 2 * t + 2)
+
+    every(lambda r: integrate(odd_ref, r))
 
     col = iota((8, RAYS), 1)
     lane_fv = bits(col, 5, 3)

time: 108 us -> 107 us (level)
  no operation moved by 1% of the time
where the time goes in v7:
time: 107 us
  blocking collectives  59.3 us (55%)
  Pallas kernels  43.6 us (41%)
  starting transfers between devices  1.95 us (2%)
  waiting for transfers between devices  1.16 us (1%)
    all_to_all x2, blocking collectives, exchange(): return lax.all_to_all(blocks, axes, split_axis=0, concat_axis=0, tiled=True)  59.3 us
    pallas_call x1, Pallas kernels, render(): pl.pallas_call(render_kernel, in_specs=[smem] + [hbm] * 9, out_specs=pl.B...  38.1 us
    pallas_call x1, Pallas kernels, composite(): pl.pallas_call(composite_kernel, in_specs=[smem, smem, smem, vmem], out_s...  4.04 us
  transfers between devices with their start and end apart: 1, of which 1 were waited for; matrix products, arithmetic and copies ran while one was open for 0% of the time, Pallas kernels for 0%

profile of v7, /device:TPU:1, one launch (start us, length us, event | category | flops | bytes accessed | tf_op | source)
XLA Modules:
  0.0 106.7 jit_solution(10067944360022257829)
XLA Ops:
  0.7 0.0 copy-start
  0.7 0.0 copy-start.1
  0.7 38.1 %render.1 = bf16[2560,128]{1,0:T(8,128)(2,1)} custom-call(s32[1]{0:T(128)} %bitcast.1.me_ref, f32[2]{0:T(128)} %bitcast.18, f32[1,1]{1,0:T(1,128)S(6)} %copy.11.rate_hbm, f32[3]{0:T(128)} %slope_hbm.1, f32[3]{0:T(128)} %bias_hbm.1, s32[16]{0:T(128)} %bitcast.19, s32[16]{0:T(128)} %bitcast.20, s32[16]{0:T(128)} %owner_ref.1, s32[16,16]{1,0:T(8,128)} %bitcast.17, ...), custom_call_target="tpu_custom_call" | custom-call | flops 4000000000 | bytes 5000000 | tf_op jit(solution)/shard_map/render/pallas_call | solution.py:253
  38.8 39.8 %all_to_all.10 = bf16[256,5,2,128]{3,2,1,0:T(2,128)(2,1)S(1)} all-to-all(bf16[256,5,2,128]{3,2,1,0:T(2,128)(2,1)} %bitcast.15), channel_id=1, replica_groups=mesh['tile'=16,'chip'=8,'core'=2] {'tile','chip','core'}, dimensions={0} | all-to-all | bytes 1310720 | tf_op jit(solution)/shard_map/all_to_all | solution.py:389
  78.5 0.0 copy-done
  78.5 0.0 copy-done.1
  78.5 4.0 %composite.1 = bf16[16,8,8,128]{3,2,1,0:T(8,128)(2,1)S(1)} custom-call(s32[1]{0:T(128)} %bitcast.1.me_ref, s32[16]{0:T(128)S(1)} %copy-done, s32[16]{0:T(128)S(1)} %copy-done.1, bf16[2560,128]{1,0:T(8,128)(2,1)S(1)} %bitcast.11), custom_call_target="tpu_custom_call" | custom-call | flops 1000000000 | bytes 1000000 | tf_op jit(solution)/shard_map/composite/pallas_call | solution.py:335
  82.6 19.6 %all_to_all.11 = bf16[128,8,128]{2,1,0:T(8,128)(2,1)S(1)} all-to-all(bf16[128,8,128]{2,1,0:T(8,128)(2,1)S(1)} %bitcast.14), channel_id=1, replica_groups=mesh['tile'=16,'chip'=8,'core'=2] {'tile','chip'}, dimensions={0} | all-to-all | bytes 524288 | tf_op jit(solution)/shard_map/all_to_all | solution.py:389
  102.1 2.0 %collective-permute-start = (bf16[1024,128]{1,0:T(8,128)(2,1)S(1)}, bf16[1024,128]{1,0:T(8,128)(2,1)S(1)}, u32[]{:S(2)}, u32[]{:S(2)}) collective-permute-start(bf16[1024,128]{1,0:T(8,128)(2,1)S(1)} %bitcast.12), channel_id=1, source_target_pairs={{0,1},{1,0},{2,3},{3,2},{4,5},{5,4},{6,7},{7,6},{8,9},{9,8},{10,11... | collective-permute-start | bytes 786440 | tf_op jit(solution)/shard_map/ppermute | solution.py:412
  104.1 1.2 %collective-permute-done.other_ref = bf16[1024,128]{1,0:T(8,128)(2,1)S(1)} collective-permute-done((bf16[1024,128]{1,0:T(8,128)(2,1)S(1)}, bf16[1024,128]{1,0:T(8,128)(2,1)S(1)}, u32[]{:S(2)}, u32[]{:S(2)}) %collective-permute-start) | collective-permute-done | bytes 262176 | tf_op jit(solution)/shard_map/ppermute | solution.py:412
  105.3 1.5 %assemble.1 = bf16[1,4,256,256]{3,2,1,0:T(8,128)(2,1)} custom-call(s32[1]{0:T(128)} %bitcast.core_ref, bf16[1024,128]{1,0:T(8,128)(2,1)S(1)} %bitcast.13, bf16[1024,128]{1,0:T(8,128)(2,1)S(1)} %collective-permute-done.other_ref), custom_call_target="tpu_custom_call" | custom-call | flops 1000000000 | bytes 1000000 | tf_op jit(solution)/shard_map/assemble/pallas_call | solution.py:376
Async XLA Ops:
  0.7 77.9 %copy-start = (s32[16]{0:T(128)S(1)}, s32[16]{0:T(128)}, u32[]{:S(2)}) copy-start(s32[16]{0:T(128)} %owner_ref.1) | copy-start | bytes 196
  0.7 77.8 %copy-start.1 = (s32[16]{0:T(128)S(1)}, s32[16]{0:T(128)}, u32[]{:S(2)}) copy-start(s32[16]{0:T(128)} %view_ref.1) | copy-start | bytes 196
  102.1 3.1 %collective-permute-start = (bf16[1024,128]{1,0:T(8,128)(2,1)S(1)}, bf16[1024,128]{1,0:T(8,128)(2,1)S(1)}, u32[]{:S(2)}, u32[]{:S(2)}) collective-permute-start(bf16[1024,128]{1,0:T(8,128)(2,1)S(1)} %bitcast.12), channel_id=1, source_target_pairs={{0,1},{1,0},{2,3},{3,2},{4,5},{5,4},{6,7},{7,6},{8,9},{9,8},{10,11... | collective-permute-start | bytes 786440 | tf_op jit(solution)/shard_map/ppermute | solution.py:412
